TPU v7x, 512 devices: a whole 4x4x16 slice. The times are simulated.
512 devices in a mesh: row: 32 (over y, x, core), col: 16 (over z).
Axes of the slice: x: 4, y: 4, z: 16, core: 2. Of those that a mesh axis runs over, the one named last changes fastest.
Arguments:
- noise: bfloat16 [16384, 128], P('row'), may hold values from -6 to 6
- w_first: bfloat16 [128, 512], replicated, may hold values from -0.5 to 0.5
- w_second: bfloat16 [512, 1024], replicated, may hold values from -0.25 to 0.25
- history: bfloat16 [16384, 1024], P('col'), may hold values from -4 to 4
Outputs:
- grad_first: float32 [128, 512], replicated
- grad_second: float32 [512, 1024], P(None, 'col')
All inputs are finite; a program needn't handle non-finite values.
Results may differ from a plain program's by a relative error of at most 0.00085.
Values sent between devices are 32-bit elements; how exact they have to be, the bound alone decides.
A program may use at most 64 MiB of HBM per device.

v0:
```python
import math

import jax
import jax.numpy as jnp
from jax import lax
from jax.sharding import PartitionSpec as P

SWEEPS = 3


EPSILON = 0.01


def row_lse(scores):
    maxima = lax.pmax(jnp.max(scores, axis=1), "col")
    totals = lax.psum(jnp.sum(jnp.exp(scores - maxima[:, None]), axis=1), "col")
    return maxima + jnp.log(totals)


def col_lse(scores):
    maxima = lax.pmax(jnp.max(scores, axis=0), "row")
    totals = lax.psum(jnp.sum(jnp.exp(scores - maxima[None, :]), axis=0), "row")
    return maxima + jnp.log(totals)


def shards(noise, w_first, w_second, history):
    gen_total = noise.shape[0] * lax.axis_size("row")
    hist_total = history.shape[0] * lax.axis_size("col")
    width = w_second.shape[1]
    slice_width = width // lax.axis_size("col")
    col_start = lax.axis_index("col") * slice_width
    preact = jnp.dot(noise, w_first, preferred_element_type=jnp.float32)
    hidden = jax.nn.silu(preact).astype(jnp.bfloat16)
    surface = jnp.dot(hidden, w_second, preferred_element_type=jnp.float32).astype(jnp.bfloat16)
    surf_f = surface.astype(jnp.float32)
    hist_f = history.astype(jnp.float32)
    surf_sq = jnp.sum(surf_f * surf_f, axis=1)
    hist_sq = jnp.sum(hist_f * hist_f, axis=1)
    inner = lax.dot_general(
        surface, history, (((1,), (1,)), ((), ())), preferred_element_type=jnp.float32
    )
    cost_tile = (surf_sq[:, None] + hist_sq[None, :] - 2.0 * inner) / width
    f_pot = jnp.zeros((noise.shape[0],), jnp.float32)
    g_pot = jnp.zeros((history.shape[0],), jnp.float32)
    for sweep_no in range(SWEEPS):
        g_pot = -EPSILON * (-math.log(gen_total) + col_lse((f_pot[:, None] - cost_tile) / EPSILON))
        f_pot = -EPSILON * (-math.log(hist_total) + row_lse((g_pot[None, :] - cost_tile) / EPSILON))
    weights = (
        jnp.exp((f_pot[:, None] + g_pot[None, :] - cost_tile) / EPSILON) / hist_total
    ).astype(jnp.bfloat16)
    partial_value = jnp.dot(weights, history, preferred_element_type=jnp.float32)
    scale = 1.0 / math.sqrt(gen_total)
    barycentre = lax.psum(partial_value, "col")
    d_surface = ((surf_f - barycentre) * scale).astype(jnp.bfloat16)
    d_hidden = lax.dot_general(
        d_surface, w_second, (((1,), (1,)), ((), ())), preferred_element_type=jnp.float32
    )
    d_slice = lax.dynamic_slice_in_dim(d_surface, col_start, slice_width, 1)
    sigma = jax.nn.sigmoid(preact)
    d_preact = (d_hidden * sigma * (1.0 + preact * (1.0 - sigma))).astype(jnp.bfloat16)
    first_term = lax.dot_general(
        noise, d_preact, (((0,), (0,)), ((), ())), preferred_element_type=jnp.float32
    )
    second_term = lax.dot_general(
        hidden, d_slice, (((0,), (0,)), ((), ())), preferred_element_type=jnp.float32
    )
    grad_first, grad_second = lax.psum((first_term, second_term), "row")
    return (grad_first, grad_second)


def solution(mesh):
    placed = (P("row", None), P(), P(), P("col", None))
    return jax.shard_map(
        shards, mesh=mesh, in_specs=placed, out_specs=(P(), P(None, "col")), check_vma=False
    )
```

profile of v0, /device:TPU:1, one launch (start us, length us, event | category | flops | bytes accessed | tf_op | source)
XLA Modules:
  0.0 862.4 jit_solution(6891692069466334634)
XLA Ops:
  7.2 0.0 copy-start
  7.2 0.0 copy-start.7
  7.2 0.0 copy-start.6
  7.2 0.0 all-reduce.4.cloned.1.call-start
  7.2 2.2 multiply_reduce_fusion
  9.4 0.0 copy-done.7
  9.4 0.0 copy-done.6
  9.4 1.3 multiply_convert_fusion.2
  10.8 0.0 copy-done
  10.8 0.8 fusion
  11.6 0.0 copy-done.4
  11.6 1.0 copy-done.1
  12.5 1.5 fusion.3
  14.1 68.9 %pmax.42 = f32[1024]{0:T(1024)S(1)} all-reduce(f32[1024]{0:T(1024)S(1)} %get-tuple-element.10), channel_id=1, replica_groups=mesh['row'=32,'col'=16] {'row'}, use_global_device_ids=true, to_apply=%region_3.4 | all-reduce | flops 1024 | bytes 8192 | tf_op jit(solution)/shard_map/pmax | solution.py:21
  83.0 0.4 exponential_reduce_fusion.5
  83.4 62.7 %psum.63 = f32[1024]{0:T(1024)S(1)} all-reduce(f32[1024]{0:T(1024)S(1)} %exponential_reduce_fusion.5), channel_id=1, replica_groups=mesh['row'=32,'col'=16] {'row'}, use_global_device_ids=true, to_apply=%region_5.6 | all-reduce | flops 1024 | bytes 8192 | tf_op jit(solution)/shard_map/psum | solution.py:22
  146.1 0.3 fusion.4
  146.4 28.8 %pmax.43 = f32[512]{0:T(512)S(1)} all-reduce(f32[512]{0:T(512)S(1)} %fusion.4), channel_id=1, replica_groups=mesh['row'=32,'col'=16] {'col'}, use_global_device_ids=true, to_apply=%region_7.8 | all-reduce | flops 512 | bytes 4096 | tf_op jit(solution)/shard_map/pmax | solution.py:15
  175.2 0.6 exponential_reduce_fusion.4
  175.7 20.1 %psum.64 = f32[512]{0:T(512)S(1)} all-reduce(f32[512]{0:T(512)S(1)} %exponential_reduce_fusion.4), channel_id=1, replica_groups=mesh['row'=32,'col'=16] {'col'}, use_global_device_ids=true, to_apply=%region_9.10 | all-reduce | flops 512 | bytes 4096 | tf_op jit(solution)/shard_map/psum | solution.py:16
  195.8 0.3 fusion.5
  196.1 76.7 %pmax.44 = f32[1024]{0:T(1024)S(1)} all-reduce(f32[1024]{0:T(1024)S(1)} %fusion.5), channel_id=1, replica_groups=mesh['row'=32,'col'=16] {'row'}, use_global_device_ids=true, to_apply=%region_11.12 | all-reduce | flops 1024 | bytes 8192 | tf_op jit(solution)/shard_map/pmax | solution.py:21
  272.8 0.5 exponential_reduce_fusion.3
  273.3 62.7 %psum.65 = f32[1024]{0:T(1024)S(1)} all-reduce(f32[1024]{0:T(1024)S(1)} %exponential_reduce_fusion.3), channel_id=1, replica_groups=mesh['row'=32,'col'=16] {'row'}, use_global_device_ids=true, to_apply=%region_13.14 | all-reduce | flops 1024 | bytes 8192 | tf_op jit(solution)/shard_map/psum | solution.py:22
  335.9 0.3 fusion.6
  336.2 22.0 %pmax.45 = f32[512]{0:T(512)S(1)} all-reduce(f32[512]{0:T(512)S(1)} %fusion.6), channel_id=1, replica_groups=mesh['row'=32,'col'=16] {'col'}, use_global_device_ids=true, to_apply=%region_15.16 | all-reduce | flops 512 | bytes 4096 | tf_op jit(solution)/shard_map/pmax | solution.py:15
  358.2 0.6 exponential_reduce_fusion.2
  358.8 20.1 %psum.66 = f32[512]{0:T(512)S(1)} all-reduce(f32[512]{0:T(512)S(1)} %exponential_reduce_fusion.2), channel_id=1, replica_groups=mesh['row'=32,'col'=16] {'col'}, use_global_device_ids=true, to_apply=%region_17.18 | all-reduce | flops 512 | bytes 4096 | tf_op jit(solution)/shard_map/psum | solution.py:16
  378.9 0.3 fusion.7
  379.2 76.7 %pmax.46 = f32[1024]{0:T(1024)S(1)} all-reduce(f32[1024]{0:T(1024)S(1)} %fusion.7), channel_id=1, replica_groups=mesh['row'=32,'col'=16] {'row'}, use_global_device_ids=true, to_apply=%region_19.20 | all-reduce | flops 1024 | bytes 8192 | tf_op jit(solution)/shard_map/pmax | solution.py:21
  455.8 0.5 exponential_reduce_fusion.1
  456.3 62.7 %psum.67 = f32[1024]{0:T(1024)S(1)} all-reduce(f32[1024]{0:T(1024)S(1)} %exponential_reduce_fusion.1), channel_id=1, replica_groups=mesh['row'=32,'col'=16] {'row'}, use_global_device_ids=true, to_apply=%region_21.22 | all-reduce | flops 1024 | bytes 8192 | tf_op jit(solution)/shard_map/psum | solution.py:22
  519.0 0.3 fusion.8
  519.3 22.0 %pmax.47 = f32[512]{0:T(512)S(1)} all-reduce(f32[512]{0:T(512)S(1)} %fusion.8), channel_id=1, replica_groups=mesh['row'=32,'col'=16] {'col'}, use_global_device_ids=true, to_apply=%region_23.24 | all-reduce | flops 512 | bytes 4096 | tf_op jit(solution)/shard_map/pmax | solution.py:15
  541.3 0.6 exponential_reduce_fusion
  541.9 20.1 %psum.68 = f32[512]{0:T(512)S(1)} all-reduce(f32[512]{0:T(512)S(1)} %exponential_reduce_fusion), channel_id=1, replica_groups=mesh['row'=32,'col'=16] {'col'}, use_global_device_ids=true, to_apply=%region_25.26 | all-reduce | flops 512 | bytes 4096 | tf_op jit(solution)/shard_map/psum | solution.py:16
  562.0 4.2 fusion.13
  566.2 0.0 all-reduce.4.cloned.1.call-update
  566.2 0.0 all-reduce.6.cloned.1.call-start
  566.2 141.2 %all-reduce.4.cloned.1.call-done = f32[512,1024]{1,0:T(8,128)} async-done(((f32[512,1024]{1,0:T(8,128)}), f32[512,1024]{1,0:T(8,128)}) %all-reduce.4.cloned.1.call-update) | async-done | bytes 2097168 | tf_op jit(solution)/shard_map/psum | solution.py:53
  707.5 0.0 copy-done.3
  707.5 2.0 fusion.2
  709.5 1.0 fusion.22
  710.5 3.1 fusion.12
  713.6 0.0 all-reduce.6.cloned.1.call-update
  713.6 138.6 %all-reduce.6.cloned.1.call-done = (f32[128,512]{0,1:T(8,128)}, f32[512,64]{0,1:T(8,128)}) async-done(((f32[128,512]{0,1:T(8,128)}, f32[512,64]{0,1:T(8,128)}), (f32[128,512]{0,1:T(8,128)}, f32[512,64]{0,1:T(8,128)})) %all-reduce.6.cloned.1.call-update) | async-done | bytes 393232 | tf_op jit(solution)/shard_map/psum | solution.py:67
  852.2 1.8 copy.6
  854.0 1.6 copy.10
  (13 shorter events, 0.1 us)
Async XLA Ops:
  7.2 3.6 copy-start
  7.2 2.2 copy-start.7
  7.2 2.2 copy-start.6
  7.2 700.3 %all-reduce.4.cloned.1.call-start = ((), (), s32[]{:S(2)}) async-start(), calls=%async_computation | async-start | bytes 4194304 | tf_op jit(solution)/shard_map/psum | solution.py:53
  10.8 0.8 copy-start.4
  10.8 1.8 copy-start.1
  11.6 2.5 copy-start.2
  566.2 141.3 %copy-start.3 = (bf16[512,1024]{1,0:T(8,128)(2,1)S(1)}, bf16[512,1024]{1,0:T(8,128)(2,1)}, u32[]{:S(2)}) copy-start(bf16[512,1024]{1,0:T(8,128)(2,1)} %copy-done.2) | copy-start | bytes 3145732
  566.2 286.0 %all-reduce.6.cloned.1.call-start = ((), (), s32[]{:S(2)}) async-start(), calls=%async_computation.1 | async-start | bytes 786432 | tf_op jit(solution)/shard_map/psum | solution.py:67
  707.5 2.0 copy-start.5
Sparse Core Ops, SparseCore 0:
  566.3 141.1 all-reduce.3
  713.7 138.3 all-reduce.5
where the time goes:
time: 863 us; the launch traced here: 862 us
  blocking collectives  543 us (63%)
  waiting for transfers between devices  280 us (32%)
  between operations  14.2 us (2%)
  matrix products  12 us (1%)
  other arithmetic  8.78 us (1%)
    pmax x3, blocking collectives, col_lse(): maxima = lax.pmax(jnp.max(scores, axis=0), 'row')  222 us
    psum x3, blocking collectives, col_lse(): totals = lax.psum(jnp.sum(jnp.exp(scores - maxima[None, :]), axis=0), 'row')  188 us
    psum x1, waiting for transfers between devices, shards(): barycentre = lax.psum(partial_value, 'col')  141 us
    psum x1, waiting for transfers between devices, shards(): grad_first, grad_second = lax.psum((first_term, second_term), 'row')  139 us
    pmax x3, blocking collectives, row_lse(): maxima = lax.pmax(jnp.max(scores, axis=1), 'col')  72.8 us
    psum x3, blocking collectives, row_lse(): totals = lax.psum(jnp.sum(jnp.exp(scores - maxima[:, None]), axis=1), 'col')  60.2 us
  transfers between devices with their start and end apart: 2, of which 2 were waited for; matrix products, arithmetic and copies ran while one was open for 0% of the time, Pallas kernels for 0%

commit v1 on v0

v1 whole, which is shorter than its diff:
```python
import functools
import math
from types import SimpleNamespace

import jax
import jax.numpy as jnp
from jax import lax
from jax.experimental import pallas as pl
from jax.experimental.pallas import tpu as pltpu
from jax.sharding import PartitionSpec as P

SWEEPS = 3
EPSILON = 0.01
MESH = pl.DeviceIdType.MESH
F32 = jnp.float32
BF16 = jnp.bfloat16
LANES = 128
CHUNK = 32


def kernel(geometry, names, noise, w_first, w_second, history, out_first, out_second, *scratch):
    ny, nx, nz = geometry
    chips = ny * nx
    n_row, n_col = 2 * chips, nz
    s = SimpleNamespace(**dict(zip(names, scratch)))
    sem = scratch[-1]
    gen, zdim = noise.shape
    hist, width = history.shape
    hid = w_first.shape[1]
    half = hid // 2
    quarter = half // 2
    gen_total, hist_total = gen * n_row, hist * n_col
    scale = 1.0 / math.sqrt(gen_total)

    me = lax.axis_index("row")
    z = lax.axis_index("col")
    core = lax.rem(me, 2)
    other = 1 - core
    chip = me // 2
    x = lax.rem(chip, nx)
    y = chip // nx
    odd = lax.rem(z, 2) == 1

    barrier = pltpu.get_barrier_semaphore()

    def greet_row(k, c):
        pl.semaphore_signal(barrier, inc=1, device_id=(lax.rem(me + k, n_row), z), device_id_type=MESH)
        return c

    def greet_col(k, c):
        pl.semaphore_signal(barrier, inc=1, device_id=(me, lax.rem(z + k, n_col)), device_id_type=MESH)
        return c

    lax.fori_loop(1, n_row, greet_row, 0)
    lax.fori_loop(1, n_col, greet_col, 0)

    def start(src, dst, number, device):
        pltpu.make_async_remote_copy(
            src_ref=src, dst_ref=dst, send_sem=sem.at[2 * number], recv_sem=sem.at[2 * number + 1],
            device_id=device, device_id_type=MESH,
        ).start()

    def wait_bytes(like, index):
        pltpu.make_async_copy(like, like, sem.at[index]).wait()

    pending = []

    def arrived(number, *like):
        for part in like:
            wait_bytes(part, 2 * number + 1)
        pending.append((number, like))

    def to_row(src, dst, number):
        def step(k, c):
            start(src, dst.at[k - 1], number, (lax.rem(me + k, n_row), z))
            return c
        lax.fori_loop(1, n_row, step, 0)

    def to_col(src, dst, number):
        def step(k, c):
            start(src, dst.at[k - 1], number, (me, lax.rem(z + k, n_col)))
            return c
        lax.fori_loop(1, n_col, step, 0)

    def at(offset, size, unit):
        return pl.ds(pl.multiple_of(offset, unit), size)

    def each(count, body):
        lax.fori_loop(0, count, lambda k, c: (body(k), c)[1], 0)

    def wide(v, copies):
        return jnp.concatenate([v] * copies, axis=1)

    def eye():
        return lax.broadcasted_iota(jnp.int32, (LANES, LANES), 0) == lax.broadcasted_iota(
            jnp.int32, (LANES, LANES), 1)

    def rows_from_line(line, dst):
        for k in range(dst.shape[0]):
            dst[k:k + 1, :] = line[:, k * LANES:(k + 1) * LANES]

    def line_from_rows(rows):
        return jnp.concatenate([rows[k:k + 1, :] for k in range(rows.shape[0])], axis=1)

    def rows_from_column(column, dst):
        for k in range(dst.shape[0]):
            block = column[k * LANES:(k + 1) * LANES, :]
            dst[k:k + 1, :] = jnp.sum(jnp.where(eye(), block, 0.0), axis=0, keepdims=True)

    def column_from_rows(rows, column):
        for k in range(rows.shape[0]):
            block = jnp.where(eye(), jnp.broadcast_to(rows[k:k + 1, :], (LANES, LANES)), 0.0)
            column[k * LANES:(k + 1) * LANES, :] = jnp.broadcast_to(
                jnp.sum(block, axis=1, keepdims=True), (LANES, LANES))

    def dot(a, b):
        return jnp.dot(a, b, preferred_element_type=F32)

    def dot_t(a, b):
        return lax.dot_general(a, b, (((1,), (1,)), ((), ())), preferred_element_type=F32)

    tile_h = min(256, hid)
    tile_g = min(256, width)
    tile_j = min(256, hist)

    s.noise_t[...] = jnp.transpose(noise[...].astype(F32)).astype(BF16)
    for n in range(hid // tile_h):
        cols = slice(n * tile_h, (n + 1) * tile_h)
        preact = dot(noise[...], w_first[:, cols])
        sigma = 1.0 / (1.0 + jnp.exp(-preact))
        hidden = preact * sigma
        s.hidden[:, cols] = hidden.astype(BF16)
        s.mult[:, cols] = sigma * (1.0 + preact * (1.0 - sigma))

    def surface_tile(n):
        cols = at(n * tile_g, tile_g, tile_g)
        s.surface[:, cols] = dot(s.hidden[...], w_second[:, cols]).astype(BF16)
    each(width // tile_g, surface_tile)

    def surf_squares(k):
        rows = at(k * CHUNK, CHUNK, CHUNK)
        v = s.surface[rows, :].astype(F32)
        total = jnp.sum(v * v, axis=1, keepdims=True)
        s.surf_sq[rows, :] = jnp.broadcast_to(total, (CHUNK, LANES))
    each(gen // CHUNK, surf_squares)

    def hist_squares(k):
        rows = at(k * LANES, LANES, LANES)
        v = history[rows, :].astype(F32)
        total = jnp.sum(v * v, axis=1, keepdims=True)
        block = jnp.where(eye(), jnp.broadcast_to(total, (LANES, LANES)), 0.0)
        s.hist_sq[:, rows] = jnp.sum(block, axis=0, keepdims=True)
    each(hist // LANES, hist_squares)

    def cost_tile(n):
        cols = at(n * tile_j, tile_j, tile_j)
        inner = dot_t(s.surface[...], history[cols, :])
        cost = (wide(s.surf_sq[...], tile_j // LANES) + s.hist_sq[:, cols] - 2.0 * inner) / width
        scores = -cost / EPSILON
        s.plan[:, cols] = scores
        top = jnp.max(scores, axis=0, keepdims=True)
        s.col_a[:, cols] = top
        s.col_b[:, cols] = jnp.sum(jnp.exp(scores - top), axis=0, keepdims=True)
    each(hist // tile_j, cost_tile)

    rows_from_line(s.col_a[...], s.m_pair.at[0])
    rows_from_line(s.col_b[...], s.m_pair.at[1])

    pl.semaphore_wait(barrier, n_row - 1 + n_col - 1)
    to_row(s.m_pair, s.m_pair_in, 0)

    def hist_w_tile(n):
        rows = at(n * 256, min(256, hist), min(256, hist))
        prod = dot_t(history[rows, :], w_second[...])
        hi = prod.astype(BF16)
        s.hist_w_hi[rows, :] = hi
        s.hist_w_lo[rows, :] = (prod - hi.astype(F32)).astype(BF16)
    each(hist // min(256, hist), hist_w_tile)

    arrived(0, s.m_pair_in)
    tops, sums = s.m_pair_in[:, 0], s.m_pair_in[:, 1]
    top = jnp.maximum(jnp.max(tops, axis=0), s.m_pair[0])
    total = jnp.sum(sums * jnp.exp(tops - top[None]), axis=0)
    total = total + s.m_pair[1] * jnp.exp(s.m_pair[0] - top)
    s.m_row[0] = math.log(gen_total) - (top + jnp.log(total))
    s.col_a[...] = line_from_rows(s.m_row[0])

    def first_rows(k):
        rows = at(k * CHUNK, CHUNK, CHUNK)
        scores = s.plan[rows, :] + s.col_a[...]
        top = jnp.max(scores, axis=1, keepdims=True)
        grown = jnp.exp(scores - top)
        s.plan[rows, :] = grown
        s.row_a[rows, :] = jnp.broadcast_to(top, (CHUNK, LANES))
        s.row_b[rows, :] = jnp.broadcast_to(jnp.sum(grown, axis=1, keepdims=True), (CHUNK, LANES))
    each(gen // CHUNK, first_rows)
    blocks = gen // LANES
    rows_from_column(s.row_a, s.m_col0.at[0])
    rows_from_column(s.row_b, s.m_col0.at[1])
    to_col(s.m_col0, s.m_col0_in, 1)

    def surf_w_tile(n):
        cols = at(n * tile_h, tile_h, tile_h)
        s.surf_w[:, cols] = dot_t(s.surface[...], w_second[cols, :])
    each(hid // tile_h, surf_w_tile)
    s.hidden_t[...] = jnp.transpose(s.hidden[...].astype(F32)).astype(BF16)

    arrived(1, s.m_col0_in)
    tops, sums = s.m_col0_in[:, 0], s.m_col0_in[:, 1]
    top = jnp.maximum(jnp.max(tops, axis=0), s.m_col0[0])
    total = jnp.sum(sums * jnp.exp(tops - top[None]), axis=0)
    total = total + s.m_col0[1] * jnp.exp(s.m_col0[0] - top)
    column_from_rows(jnp.exp(s.m_col0[0] - top) / total, s.row_a)

    def column_sums(scaled):
        def step(k, acc):
            rows = at(k * CHUNK, CHUNK, CHUNK)
            v = s.plan[rows, :] * wide(s.row_a[rows, :], hist // LANES)
            if scaled:
                s.plan[rows, :] = v
            return acc + jnp.sum(v.reshape(CHUNK // 8, 8, hist), axis=0)
        acc = lax.fori_loop(0, gen // CHUNK, step, jnp.zeros((8, hist), F32))
        return jnp.sum(acc, axis=0, keepdims=True)

    def row_sums(k):
        rows = at(k * CHUNK, CHUNK, CHUNK)
        v = jnp.sum(s.plan[rows, :] * s.col_a[...], axis=1, keepdims=True)
        s.row_b[rows, :] = jnp.broadcast_to(v, (CHUNK, LANES))

    for sweep in range(1, SWEEPS):
        number = 2 * sweep
        mine, theirs = s.m_row.at[sweep], s.m_row_in.at[sweep - 1]
        rows_from_line(column_sums(sweep == 1), mine)
        to_row(mine, theirs, number)
        if sweep == 1:
            pair = at(lax.div(z, 2) * LANES, LANES, LANES)
            prod = dot(s.hidden_t[...], s.surface[:, pair])
            turned = pltpu.roll(prod, 64, axis=1)
            s.term_a[...] = jnp.where(odd, turned, prod)
            s.term_b[...] = jnp.where(odd, prod, turned)
            low = lax.broadcasted_iota(jnp.int32, (8, LANES), 1) < 64

            def owner_term(o):
                oc, ox, oy = lax.rem(o, 2), lax.rem(o // 2, nx), o // (2 * nx)
                upper = oc * half + ox * (quarter // nx) + oy * 8
                lower = oc * half + quarter + oy * (quarter // ny) + ox * 8
                s.term[o] = jnp.where(
                    low, s.term_a[at(upper, 8, 8), :], s.term_b[at(lower, 8, 8), :])
            each(n_row, owner_term)

            def send_term(k, c):
                peer = lax.rem(me + k, n_row)
                start(s.term.at[peer], s.term_in.at[k - 1], 6, (peer, z))
                return c
            lax.fori_loop(1, n_row, send_term, 0)
        arrived(number, theirs)
        total = mine[...] + jnp.sum(theirs[...], axis=0)
        s.col_a[...] = line_from_rows((gen_total / hist_total) / total)

        each(gen // CHUNK, row_sums)
        mine, theirs = s.m_col.at[sweep - 1], s.m_col_in.at[sweep - 1]
        rows_from_column(s.row_b, mine)
        to_col(mine, theirs, number + 1)
        arrived(number + 1, theirs)
        total = mine[...] + jnp.sum(theirs[...], axis=0)
        column_from_rows(1.0 / total, s.row_a)

    def weight_rows(k):
        rows = at(k * CHUNK, CHUNK, CHUNK)
        v = s.plan[rows, :] * wide(s.row_a[rows, :], hist // LANES) * s.col_a[...]
        s.weights[rows, :] = v.astype(BF16)
    each(gen // CHUNK, weight_rows)

    def acc_tile(which):
        rows = at(which * half, half, half)

        def body(n):
            cols = at(n * tile_j, tile_j, tile_j)
            s.acc[rows, cols] = dot(s.hidden_t[rows, :], s.weights[:, cols])
        each(hist // tile_j, body)

    sibling = (me + 1 - 2 * core, z)
    acc_tile(other)
    start(s.acc.at[at(other * half, half, half), :], s.acc_in, 7, sibling)
    acc_tile(core)

    def first_tile(n):
        cols = at(n * tile_h, tile_h, tile_h)
        value = dot(s.weights[...], s.hist_w_hi[:, cols]) + dot(s.weights[...], s.hist_w_lo[:, cols])
        d_hidden = (s.surf_w[:, cols] * (1.0 / n_col) - value) * scale
        d_preact = d_hidden * s.mult[:, cols]
        hi = d_preact.astype(BF16)
        lo = (d_preact - hi.astype(F32)).astype(BF16)
        s.first[:, cols] = dot(s.noise_t[...], hi) + dot(s.noise_t[...], lo)
    each(hid // tile_h, first_tile)
    start(s.first.at[:, at(other * half, half, half)], s.first_in, 8, sibling)

    arrived(7, s.acc_in)

    def add_sibling(k):
        rows = at(core * half + k * CHUNK, CHUNK, CHUNK)
        s.acc[rows, :] = s.acc[rows, :] + s.acc_in[at(k * CHUNK, CHUNK, CHUNK), :]
    each(half // CHUNK, add_sibling)
    span_x, span_y = quarter // nx, quarter // ny
    base_u, base_l = core * half, core * half + quarter
    for k in range(1, nx):
        to = lax.rem(x + k, nx)
        start(s.acc.at[at(base_u + to * span_x, span_x, 8), :], s.x_in.at[k - 1], 9,
              ((y * nx + to) * 2 + core, z))
    for k in range(1, ny):
        to = lax.rem(y + k, ny)
        start(s.acc.at[at(base_l + to * span_y, span_y, 8), :], s.y_in.at[k - 1], 10,
              ((to * nx + x) * 2 + core, z))

    arrived(8, s.first_in)
    s.first_half[...] = s.first[:, at(core * half, half, half)] + s.first_in[...]
    piece = zdim // chips

    def send_first(k, c):
        to = lax.rem(chip + k, chips)
        start(s.first_half.at[at(to * piece, piece, 8), :], s.first_chip_in.at[k - 1], 11,
              (to * 2 + core, z))
        return c
    lax.fori_loop(1, chips, send_first, 0)
    arrived(11, s.first_chip_in)
    s.first_piece[0] = s.first_half[at(chip * piece, piece, 8), :] + jnp.sum(s.first_chip_in[...], axis=0)
    to_col(s.first_piece.at[0], s.first_z_in, 12)

    arrived(9, s.x_in)
    arrived(10, s.y_in)
    rows_u, rows_l = at(base_u + x * span_x, span_x, 8), at(base_l + y * span_y, span_y, 8)
    s.acc[rows_u, :] = s.acc[rows_u, :] + jnp.sum(s.x_in[...], axis=0)
    s.acc[rows_l, :] = s.acc[rows_l, :] + jnp.sum(s.y_in[...], axis=0)
    for k in range(1, ny):
        to = lax.rem(y + k, ny)
        start(s.acc.at[at(base_u + x * span_x + to * 8, 8, 8), :], s.y_in2.at[k - 1], 13,
              ((to * nx + x) * 2 + core, z))
    for k in range(1, nx):
        to = lax.rem(x + k, nx)
        start(s.acc.at[at(base_l + y * span_y + to * 8, 8, 8), :], s.x_in2.at[k - 1], 14,
              ((y * nx + to) * 2 + core, z))
    arrived(13, s.y_in2)
    arrived(14, s.x_in2)
    mine_u, mine_l = base_u + x * span_x + y * 8, base_l + y * span_y + x * 8
    s.reduced[0:8, :] = s.acc[at(mine_u, 8, 8), :] + jnp.sum(s.y_in2[...], axis=0)
    s.reduced[8:16, :] = s.acc[at(mine_l, 8, 8), :] + jnp.sum(s.x_in2[...], axis=0)

    hi = s.reduced[...].astype(BF16)
    lo = (s.reduced[...] - hi.astype(F32)).astype(BF16)
    both = jnp.concatenate([hi, lo], axis=0)

    def mix_tile(n):
        cols = at(n * tile_g, tile_g, tile_g)
        prod = dot(both, history[:, cols])
        s.mix[:, cols] = prod[0:16] + prod[16:32]
    each(width // tile_g, mix_tile)
    low = lax.broadcasted_iota(jnp.int32, (8, LANES), 1) < 64
    for k in range(nz):
        lanes = slice((k // 2) * LANES, (k // 2 + 1) * LANES)
        upper, lower = s.mix[0:8, lanes], s.mix[8:16, lanes]
        if k % 2 == 0:
            s.slices[k] = jnp.where(low, upper, pltpu.roll(lower, 64, axis=1))
        else:
            s.slices[k] = jnp.where(low, pltpu.roll(upper, 64, axis=1), lower)

    def send_slice(k, c):
        to = lax.rem(z + k, n_col)
        start(s.slices.at[to], s.slices_in.at[k - 1], 15, (me, to))
        return c
    lax.fori_loop(1, n_col, send_slice, 0)

    arrived(12, s.first_z_in)
    s.first_all[core, chip] = s.first_piece[0] + jnp.sum(s.first_z_in[...], axis=0)

    def spread(array, number):
        def step(k, c):
            start(array.at[core, chip], array.at[core, chip], number, (lax.rem(chip + k, chips) * 2 + core, z))
            return c
        lax.fori_loop(1, chips, step, 0)
    spread(s.first_all, 16)

    arrived(6, s.term_in)
    term = s.term[me] + jnp.sum(s.term_in[...], axis=0)
    arrived(15, s.slices_in)
    mixed = s.slices[z] + jnp.sum(s.slices_in[...], axis=0)
    s.second_all[core, chip] = (term - mixed) * scale
    spread(s.second_all, 17)

    arrived(16, s.first_all.at[0, pl.ds(0, chips - 1)])
    start(s.first_all.at[core], s.first_all.at[core], 18, sibling)
    arrived(17, s.second_all.at[0, pl.ds(0, chips - 1)])
    start(s.second_all.at[core], s.second_all.at[core], 19, sibling)
    arrived(18, s.first_all.at[0])
    arrived(19, s.second_all.at[0])

    def place_chip(k):
        for c in range(2):
            out_first[at(k * piece, piece, 8), c * half:(c + 1) * half] = s.first_all[c, k]
            cx, cy = lax.rem(k, nx), k // nx
            v = s.second_all[c, k]
            out_second[at(c * half + cx * span_x + cy * 8, 8, 8), :] = v[:, 0:64]
            out_second[at(c * half + quarter + cy * span_y + cx * 8, 8, 8), :] = pltpu.roll(v, 64, axis=1)[:, 0:64]
    each(chips, place_chip)

    for number, like in pending:
        for part in like:
            wait_bytes(part, 2 * number)


def shards(geometry, noise, w_first, w_second, history):
    ny, nx, nz = geometry
    chips = ny * nx
    n_row = 2 * chips
    gen, zdim = noise.shape
    hist, width = history.shape
    hid = w_first.shape[1]
    half, quarter = hid // 2, hid // 4
    piece = zdim // chips
    jr, ir = hist // LANES, gen // LANES
    shapes = dict(
        hidden=((gen, hid), BF16), hidden_t=((hid, gen), BF16), noise_t=((zdim, gen), BF16),
        surface=((gen, width), BF16), mult=((gen, hid), F32), surf_w=((gen, hid), F32),
        hist_w_hi=((hist, hid), BF16), hist_w_lo=((hist, hid), BF16),
        plan=((gen, hist), F32), weights=((gen, hist), BF16),
        surf_sq=((gen, LANES), F32), hist_sq=((1, hist), F32),
        row_a=((gen, LANES), F32), row_b=((gen, LANES), F32), col_a=((1, hist), F32), col_b=((1, hist), F32),
        row_col=((8, LANES), F32), row_sum=((8, LANES), F32),
        m_pair=((2, jr, LANES), F32), m_pair_in=((n_row - 1, 2, jr, LANES), F32),
        m_col0=((2, ir, LANES), F32), m_col0_in=((nz - 1, 2, ir, LANES), F32),
        m_row=((SWEEPS, jr, LANES), F32), m_row_in=((SWEEPS - 1, n_row - 1, jr, LANES), F32),
        m_col=((SWEEPS - 1, ir, LANES), F32), m_col_in=((SWEEPS - 1, nz - 1, ir, LANES), F32),
        acc=((hid, hist), F32), acc_in=((half, hist), F32),
        x_in=((nx - 1, quarter // nx, hist), F32), y_in=((ny - 1, quarter // ny, hist), F32),
        x_in2=((nx - 1, 8, hist), F32), y_in2=((ny - 1, 8, hist), F32), reduced=((16, hist), F32),
        first=((zdim, hid), F32), first_in=((zdim, half), F32), first_half=((zdim, half), F32),
        first_chip_in=((chips - 1, piece, half), F32), first_piece=((1, piece, half), F32),
        first_z_in=((nz - 1, piece, half), F32), first_all=((2, chips, piece, half), F32),
        term_a=((hid, LANES), F32), term_b=((hid, LANES), F32),
        term=((n_row, 8, LANES), F32), term_in=((n_row - 1, 8, LANES), F32),
        mix=((16, width), F32), slices=((nz, 8, LANES), F32), slices_in=((nz - 1, 8, LANES), F32),
        second_all=((2, chips, 8, LANES), F32),
    )
    scratch = [pltpu.VMEM(*shape) for shape in shapes.values()] + [pltpu.SemaphoreType.DMA((40,))]
    slice_width = width // nz
    return pl.pallas_call(
        functools.partial(kernel, geometry, tuple(shapes)),
        out_shape=(
            jax.ShapeDtypeStruct((zdim, hid), F32),
            jax.ShapeDtypeStruct((hid, slice_width), F32),
        ),
        in_specs=[pl.BlockSpec(memory_space=pltpu.VMEM)] * 4,
        out_specs=(pl.BlockSpec(memory_space=pltpu.VMEM),) * 2,
        scratch_shapes=scratch,
        compiler_params=pltpu.CompilerParams(
            collective_id=0, has_side_effects=True, vmem_limit_bytes=56 * 1024 * 1024
        ),
        name="transport",
    )(noise, w_first, w_second, history)


def solution(mesh):
    chips = mesh.shape["row"] // 2
    nx = math.isqrt(chips)
    geometry = (chips // nx, nx, mesh.shape["col"])
    placed = (P("row", None), P(), P(), P("col", None))
    return jax.shard_map(
        functools.partial(shards, geometry), mesh=mesh, in_specs=placed,
        out_specs=(P(), P(None, "col")), check_vma=False,
    )
```

time: 863 us -> 106 us (0.12)
  blocking collectives: 543 us -> 0 us
  waiting for transfers between devices: 280 us -> 0 us
  Pallas kernels: 0 us -> 102 us
  between operations: 14.2 us -> 0.64 us
  matrix products: 12 us -> 0 us
  other arithmetic: 8.78 us -> 0 us
    pmax x6 -> x0, blocking collectives: 295 us -> none  [the longest x3 222 us: col_lse(): maxima = lax.pmax(jnp.max(scores, axis=0), 'row')]
    psum x2 -> x0, waiting for transfers between devices: 280 us -> none  [the longest x1 141 us: shards(): barycentre = lax.psum(partial_value, 'col')]
    psum x6 -> x0, blocking collectives: 248 us -> none  [the longest x3 188 us: col_lse(): totals = lax.psum(jnp.sum(jnp.exp(scores - maxima[None, :]), axis=0), 'row')]
    pallas_call x0 -> x1, Pallas kernels: none -> 102 us  [shards(): pl.pallas_call(functools.partial(kernel, geometry, tuple(shapes)), out_sh...]
    dot_general x6 -> x0, matrix products: 12 us -> none  [the longest x1 4.2 us: shards(): jnp.dot(weights, history, preferred_element_type=jnp.float32)]
  transfers between devices with their start and end apart: 2 -> 0, of which waited for: 2 -> 0; matrix products, arithmetic and copies ran while one was open for 0% -> 0% of each run, Pallas kernels for 0% -> 0%
where the time goes in v1:
time: 106 us
  Pallas kernels  102 us (96%)
  local copies, waits for them, and re-layouts  3.39 us (3%)
    pallas_call x1, Pallas kernels, shards(): pl.pallas_call(functools.partial(kernel, geometry, tuple(shapes)), out_sh...  102 us

profile of v1, /device:TPU:1, one launch (start us, length us, event | category | flops | bytes accessed | tf_op | source)
XLA Modules:
  0.0 106.0 jit_solution(3591972666542307847)
XLA Ops:
  0.6 101.9 %transport.1 = (f32[128,512]{1,0:T(8,128)}, f32[512,64]{1,0:T(8,128)}) custom-call(bf16[512,128]{1,0:T(8,128)(2,1)} %noise.1, bf16[128,512]{1,0:T(8,128)(2,1)} %w_first.1, bf16[512,1024]{1,0:T(8,128)(2,1)} %w_second.1, bf16[1024,1024]{1,0:T(8,128)(2,1)} %history.1), custom_call_target="tpu_custom_call" | custom-call | tf_op jit(solution)/shard_map/transport/pallas_call | solution.py:445
  102.6 1.7 %copy.6 = f32[512,64]{0,1:T(8,128)} copy(f32[512,64]{1,0:T(8,128)} %get-tuple-element.3) | data formatting | bytes 262144 | tf_op jit(solution)/shard_map/transport/pallas_call | solution.py:445
  104.3 1.7 %copy.8 = f32[128,512]{1,0:T(8,128)} copy(f32[128,512]{1,0:T(8,128)} %get-tuple-element.6) | data formatting | bytes 524288

commit v2 on v1

v2 whole, which is shorter than its diff:
```python
import functools
import math
from types import SimpleNamespace

import jax
import jax.numpy as jnp
from jax import lax
from jax.experimental import pallas as pl
from jax.experimental.pallas import tpu as pltpu
from jax.sharding import PartitionSpec as P

SWEEPS = 3
EPSILON = 0.01
MESH = pl.DeviceIdType.MESH
F32 = jnp.float32
BF16 = jnp.bfloat16
LANES = 128


def kernel(geometry, names, noise, w_first, w_second, history, out_first, out_second, *scratch):
    ny, nx, nz = geometry
    chips = ny * nx
    n_row, n_col = 2 * chips, nz
    s = SimpleNamespace(**dict(zip(names, scratch)))
    sem = scratch[-1]
    gen, zdim = noise.shape
    hist, width = history.shape
    hid = w_first.shape[1]
    half = hid // 2
    quarter = half // 2
    gen_total, hist_total = gen * n_row, hist * n_col
    scale = 1.0 / math.sqrt(gen_total)

    me = lax.axis_index("row")
    z = lax.axis_index("col")
    core = lax.rem(me, 2)
    other = 1 - core
    chip = me // 2
    x = lax.rem(chip, nx)
    y = chip // nx
    odd = lax.rem(z, 2) == 1

    barrier = pltpu.get_barrier_semaphore()

    def greet_row(k, c):
        pl.semaphore_signal(barrier, inc=1, device_id=(lax.rem(me + k, n_row), z), device_id_type=MESH)
        return c

    def greet_col(k, c):
        pl.semaphore_signal(barrier, inc=1, device_id=(me, lax.rem(z + k, n_col)), device_id_type=MESH)
        return c

    lax.fori_loop(1, n_row, greet_row, 0)
    lax.fori_loop(1, n_col, greet_col, 0)

    def start(src, dst, number, device):
        pltpu.make_async_remote_copy(
            src_ref=src, dst_ref=dst, send_sem=sem.at[2 * number], recv_sem=sem.at[2 * number + 1],
            device_id=device, device_id_type=MESH,
        ).start()

    def wait_bytes(like, index):
        pltpu.make_async_copy(like, like, sem.at[index]).wait()

    flying, landed = {}, {}

    def expect(number, like):
        flying[number] = like

    def arrived(number):
        landed[number] = flying.pop(number)
        wait_bytes(landed[number], 2 * number + 1)

    def finish():
        for number in tuple(flying):
            arrived(number)
        for number, like in landed.items():
            wait_bytes(like, 2 * number)

    def to_row(src, dst, number):
        def step(k, c):
            start(src, dst.at[k - 1], number, (lax.rem(me + k, n_row), z))
            return c
        lax.fori_loop(1, n_row, step, 0)
        expect(number, dst)

    def to_col(src, dst, number):
        def step(k, c):
            start(src, dst.at[k - 1], number, (me, lax.rem(z + k, n_col)))
            return c
        lax.fori_loop(1, n_col, step, 0)
        expect(number, dst)

    def at(offset, size, unit):
        return pl.ds(offset if isinstance(offset, int) else pl.multiple_of(offset, unit), size)

    def each(count, body):
        lax.fori_loop(0, count, lambda k, c: (body(k), c)[1], 0)

    tiles = [slice(k * LANES, (k + 1) * LANES) for k in range(max(hist, width) // LANES)]
    plan_tiles = tiles[:hist // LANES]
    blocks = gen // LANES

    def block(k):
        return at(k * LANES, LANES, LANES)

    def fold(v):
        return jnp.sum(v.reshape(LANES // 8, 8, LANES), axis=0)

    def rows_from_column(column, dst, total):
        for k in range(dst.shape[0]):
            turned = jnp.transpose(column[tiles[k], :])
            dst[k:k + 1, :] = jnp.sum(turned, axis=0, keepdims=True) if total else turned[0:1, :]

    def column_from_rows(rows, column):
        for k in range(rows.shape[0]):
            column[tiles[k], :] = jnp.transpose(jnp.broadcast_to(rows[k:k + 1, :], (LANES, LANES)))

    def dot(a, b):
        return jnp.dot(a, b, preferred_element_type=F32)

    def dot_t(a, b):
        return lax.dot_general(a, b, (((1,), (1,)), ((), ())), preferred_element_type=F32)

    tile_h = min(256, hid)
    tile_g = min(256, width)
    tile_j = min(256, hist)

    for n in range(hid // tile_h):
        cols = slice(n * tile_h, (n + 1) * tile_h)
        preact = dot(noise[...], w_first[:, cols])
        s.mult[:, cols] = preact
        s.hidden[:, cols] = (preact / (1.0 + jnp.exp(-preact))).astype(BF16)

    def surface_tile(n):
        cols = at(n * tile_g, tile_g, tile_g)
        s.surface[:, cols] = dot(s.hidden[...], w_second[:, cols]).astype(BF16)
    each(width // tile_g, surface_tile)

    def squares(ref, rows):
        total = jnp.zeros((LANES, LANES), F32)
        for cols in tiles[:width // LANES]:
            v = ref[rows, cols].astype(F32)
            total = total + v * v
        return total

    def surf_squares(k):
        s.surf_sq[block(k), :] = squares(s.surface, block(k))
    each(blocks, surf_squares)
    s.surf_sq[...] = jnp.broadcast_to(jnp.sum(s.surf_sq[...], axis=1, keepdims=True), (gen, LANES))

    def hist_squares(k):
        s.hist_sq[:, block(k)] = jnp.sum(jnp.transpose(squares(history, block(k))), axis=0, keepdims=True)
    each(hist // LANES, hist_squares)

    def inner_tile(n):
        cols = at(n * tile_j, tile_j, tile_j)
        s.plan[:, cols] = dot_t(s.surface[...], history[cols, :])
    each(hist // tile_j, inner_tile)

    def score_block(k, tops):
        rows, out = block(k), []
        own = s.surf_sq[rows, :]
        for cols, top in zip(plan_tiles, tops):
            cost = (own + s.hist_sq[:, cols] - 2.0 * s.plan[rows, cols]) * (1.0 / width)
            scores = cost * (-1.0 / EPSILON)
            s.plan[rows, cols] = scores
            out.append(jnp.maximum(top, jnp.max(scores.reshape(LANES // 8, 8, LANES), axis=0)))
        return tuple(out)
    tops = lax.fori_loop(0, blocks, score_block, tuple(jnp.full((8, LANES), -jnp.inf, F32) for _ in plan_tiles))
    for k, top in enumerate(tops):
        s.m_pair[0, k:k + 1, :] = jnp.max(top, axis=0, keepdims=True)

    def score_sums(k, sums):
        rows, out = block(k), []
        for n, (cols, total) in enumerate(zip(plan_tiles, sums)):
            out.append(total + fold(jnp.exp(s.plan[rows, cols] - s.m_pair[0, n:n + 1, :])))
        return tuple(out)
    zeros = tuple(jnp.zeros((8, LANES), F32) for _ in plan_tiles)
    for k, total in enumerate(lax.fori_loop(0, blocks, score_sums, zeros)):
        s.m_pair[1, k:k + 1, :] = jnp.sum(total, axis=0, keepdims=True)

    pl.semaphore_wait(barrier, n_row - 1 + n_col - 1)
    to_row(s.m_pair, s.m_pair_in, 0)

    def hist_w_tile(n):
        rows = at(n * 256, min(256, hist), min(256, hist))
        prod = dot_t(history[rows, :], w_second[...])
        hi = prod.astype(BF16)
        s.hist_w_hi[rows, :] = hi
        s.hist_w_lo[rows, :] = (prod - hi.astype(F32)).astype(BF16)
    each(hist // min(256, hist), hist_w_tile)

    arrived(0)
    tops, sums = s.m_pair_in[:, 0], s.m_pair_in[:, 1]
    top = jnp.maximum(jnp.max(tops, axis=0), s.m_pair[0])
    total = jnp.sum(sums * jnp.exp(tops - top[None]), axis=0)
    total = total + s.m_pair[1] * jnp.exp(s.m_pair[0] - top)
    s.m_row[0] = math.log(gen_total) - (top + jnp.log(total))

    def row_tops(k):
        rows = block(k)
        top = s.plan[rows, plan_tiles[0]] + s.m_row[0, 0:1, :]
        for n, cols in enumerate(plan_tiles[1:], 1):
            top = jnp.maximum(top, s.plan[rows, cols] + s.m_row[0, n:n + 1, :])
        s.row_a[rows, :] = top
    each(blocks, row_tops)
    s.row_a[...] = jnp.broadcast_to(jnp.max(s.row_a[...], axis=1, keepdims=True), (gen, LANES))

    def first_rows(k):
        rows = block(k)
        top, total = s.row_a[rows, :], jnp.zeros((LANES, LANES), F32)
        for n, cols in enumerate(plan_tiles):
            grown = jnp.exp(s.plan[rows, cols] + s.m_row[0, n:n + 1, :] - top)
            s.plan[rows, cols] = grown
            total = total + grown
        s.row_b[rows, :] = total
    each(blocks, first_rows)
    rows_from_column(s.row_a, s.m_col0.at[0], False)
    rows_from_column(s.row_b, s.m_col0.at[1], True)
    to_col(s.m_col0, s.m_col0_in, 1)

    def surf_w_tile(n):
        cols = at(n * tile_h, tile_h, tile_h)
        s.surf_w[:, cols] = dot_t(s.surface[...], w_second[cols, :])
    each(hid // tile_h, surf_w_tile)
    s.hidden_t[...] = jnp.transpose(s.hidden[...].astype(F32)).astype(BF16)

    pair = at(lax.div(z, 2) * LANES, LANES, LANES)
    prod = dot(s.hidden_t[...], s.surface[:, pair])
    turned = pltpu.roll(prod, 64, axis=1)
    s.term_a[...] = jnp.where(odd, turned, prod)
    s.term_b[...] = jnp.where(odd, prod, turned)
    low = lax.broadcasted_iota(jnp.int32, (8, LANES), 1) < 64

    def owner_term(o):
        oc, ox, oy = lax.rem(o, 2), lax.rem(o // 2, nx), o // (2 * nx)
        upper = oc * half + ox * (quarter // nx) + oy * 8
        lower = oc * half + quarter + oy * (quarter // ny) + ox * 8
        s.term[o] = jnp.where(low, s.term_a[at(upper, 8, 8), :], s.term_b[at(lower, 8, 8), :])
    each(n_row, owner_term)

    def send_term(k, c):
        peer = lax.rem(me + k, n_row)
        start(s.term.at[peer], s.term_in.at[k - 1], 6, (peer, z))
        return c
    lax.fori_loop(1, n_row, send_term, 0)
    expect(6, s.term_in)

    arrived(1)
    tops, sums = s.m_col0_in[:, 0], s.m_col0_in[:, 1]
    top = jnp.maximum(jnp.max(tops, axis=0), s.m_col0[0])
    total = jnp.sum(sums * jnp.exp(tops - top[None]), axis=0)
    total = total + s.m_col0[1] * jnp.exp(s.m_col0[0] - top)
    column_from_rows(jnp.exp(s.m_col0[0] - top) / total, s.row_a)

    def column_sums(scaled, dst):
        def step(k, sums):
            rows, out = block(k), []
            own = s.row_a[rows, :]
            for cols, total in zip(plan_tiles, sums):
                v = s.plan[rows, cols] * own
                if scaled:
                    s.plan[rows, cols] = v
                out.append(total + fold(v))
            return tuple(out)
        for k, total in enumerate(lax.fori_loop(0, blocks, step, zeros)):
            dst[k:k + 1, :] = jnp.sum(total, axis=0, keepdims=True)

    def row_sums(k):
        rows = block(k)
        total = jnp.zeros((LANES, LANES), F32)
        for n, cols in enumerate(plan_tiles):
            total = total + s.plan[rows, cols] * s.col_b[n:n + 1, :]
        s.row_b[rows, :] = total

    for sweep in range(1, SWEEPS):
        number = 2 * sweep
        mine, theirs = s.m_row.at[sweep], s.m_row_in.at[sweep - 1]
        column_sums(sweep == 1, mine)
        to_row(mine, theirs, number)
        if sweep == 1:
            preact = s.mult[...]
            sigma = 1.0 / (1.0 + jnp.exp(-preact))
            s.mult[...] = sigma * (1.0 + preact * (1.0 - sigma))
            s.noise_t[...] = jnp.transpose(noise[...].astype(F32)).astype(BF16)
        arrived(number)
        total = mine[...] + jnp.sum(theirs[...], axis=0)
        s.col_b[...] = (gen_total / hist_total) / total

        each(blocks, row_sums)
        mine, theirs = s.m_col.at[sweep - 1], s.m_col_in.at[sweep - 1]
        rows_from_column(s.row_b, mine, True)
        to_col(mine, theirs, number + 1)
        arrived(number + 1)
        total = mine[...] + jnp.sum(theirs[...], axis=0)
        column_from_rows(1.0 / total, s.row_a)

    def weight_rows(k):
        rows = block(k)
        own = s.row_a[rows, :]
        for n, cols in enumerate(plan_tiles):
            s.weights[rows, cols] = (s.plan[rows, cols] * own * s.col_b[n:n + 1, :]).astype(BF16)
    each(blocks, weight_rows)

    def acc_tile(which):
        rows = at(which * half, half, half)

        def body(n):
            cols = at(n * tile_j, tile_j, tile_j)
            s.acc[rows, cols] = dot(s.hidden_t[rows, :], s.weights[:, cols])
        each(hist // tile_j, body)

    span_x, span_y = quarter // nx, quarter // ny
    base_u, base_l = core * half, core * half + quarter
    sibling = (me + 1 - 2 * core, z)
    acc_tile(other)
    order = [pair for k in range(1, nx) for pair in ((True, k), (False, k))] + [(True, 0), (False, 0)]

    def block_rows(upper, k):
        return lax.rem(x + k, nx) * span_x if upper else quarter + lax.rem(y + k, ny) * span_y

    for n, (upper, k) in enumerate(order):
        rows = block_rows(upper, k)
        start(s.acc.at[at(other * half + rows, span_x, 8), :], s.acc_in.at[at(rows, span_x, 8), :], 20 + n, sibling)
        expect(20 + n, s.acc_in.at[at(n * span_x, span_x, 8), :])
    acc_tile(core)

    def pass_on(n):
        upper, k = order[n]
        rows = block_rows(upper, k)
        arrived(20 + n)
        mine = at(core * half + rows, span_x, 8)
        s.acc[mine, :] = s.acc[mine, :] + s.acc_in[at(rows, span_x, 8), :]
        if k and upper:
            start(s.acc.at[mine, :], s.x_in.at[k - 1], 9, ((y * nx + lax.rem(x + k, nx)) * 2 + core, z))
        elif k:
            start(s.acc.at[mine, :], s.y_in.at[k - 1], 10, ((lax.rem(y + k, ny) * nx + x) * 2 + core, z))

    def first_tile(n):
        cols = at(n * tile_h, tile_h, tile_h)
        value = dot(s.weights[...], s.hist_w_hi[:, cols]) + dot(s.weights[...], s.hist_w_lo[:, cols])
        d_hidden = (s.surf_w[:, cols] * (1.0 / n_col) - value) * scale
        d_preact = d_hidden * s.mult[:, cols]
        hi = d_preact.astype(BF16)
        lo = (d_preact - hi.astype(F32)).astype(BF16)
        s.first[:, cols] = dot(s.noise_t[...], hi) + dot(s.noise_t[...], lo)

    for n in range(2):
        pass_on(2 * n)
        pass_on(2 * n + 1)
        first_tile(n)
    start(s.first.at[:, at(other * half, half, half)], s.first_in, 8, sibling)
    expect(8, s.first_in)
    for n in range(4, len(order)):
        pass_on(n)
    expect(9, s.x_in)
    expect(10, s.y_in)

    arrived(8)
    s.first_half[...] = s.first[:, at(core * half, half, half)] + s.first_in[...]
    piece = zdim // chips

    def send_first(k, c):
        to = lax.rem(chip + k, chips)
        start(s.first_half.at[at(to * piece, piece, 8), :], s.first_chip_in.at[k - 1], 11,
              (to * 2 + core, z))
        return c
    lax.fori_loop(1, chips, send_first, 0)
    expect(11, s.first_chip_in)
    arrived(11)
    s.first_piece[0] = s.first_half[at(chip * piece, piece, 8), :] + jnp.sum(s.first_chip_in[...], axis=0)
    to_col(s.first_piece.at[0], s.first_z_in, 12)

    arrived(9)
    arrived(10)
    rows_u, rows_l = at(base_u + x * span_x, span_x, 8), at(base_l + y * span_y, span_y, 8)
    s.acc[rows_u, :] = s.acc[rows_u, :] + jnp.sum(s.x_in[...], axis=0)
    s.acc[rows_l, :] = s.acc[rows_l, :] + jnp.sum(s.y_in[...], axis=0)
    for k in range(1, ny):
        to = lax.rem(y + k, ny)
        start(s.acc.at[at(base_u + x * span_x + to * 8, 8, 8), :], s.y_in2.at[k - 1], 13,
              ((to * nx + x) * 2 + core, z))
    for k in range(1, nx):
        to = lax.rem(x + k, nx)
        start(s.acc.at[at(base_l + y * span_y + to * 8, 8, 8), :], s.x_in2.at[k - 1], 14,
              ((y * nx + to) * 2 + core, z))
    expect(13, s.y_in2)
    expect(14, s.x_in2)
    arrived(13)
    arrived(14)
    mine_u, mine_l = base_u + x * span_x + y * 8, base_l + y * span_y + x * 8
    s.reduced[0:8, :] = s.acc[at(mine_u, 8, 8), :] + jnp.sum(s.y_in2[...], axis=0)
    s.reduced[8:16, :] = s.acc[at(mine_l, 8, 8), :] + jnp.sum(s.x_in2[...], axis=0)

    hi = s.reduced[...].astype(BF16)
    lo = (s.reduced[...] - hi.astype(F32)).astype(BF16)
    both = jnp.concatenate([hi, lo], axis=0)

    def mix_tile(n):
        cols = at(n * tile_g, tile_g, tile_g)
        prod = dot(both, history[:, cols])
        s.mix[:, cols] = prod[0:16] + prod[16:32]
    each(width // tile_g, mix_tile)
    low = lax.broadcasted_iota(jnp.int32, (8, LANES), 1) < 64
    for k in range(nz):
        lanes = slice((k // 2) * LANES, (k // 2 + 1) * LANES)
        upper, lower = s.mix[0:8, lanes], s.mix[8:16, lanes]
        if k % 2 == 0:
            s.slices[k] = jnp.where(low, upper, pltpu.roll(lower, 64, axis=1))
        else:
            s.slices[k] = jnp.where(low, pltpu.roll(upper, 64, axis=1), lower)

    def send_slice(k, c):
        to = lax.rem(z + k, n_col)
        start(s.slices.at[to], s.slices_in.at[k - 1], 15, (me, to))
        return c
    lax.fori_loop(1, n_col, send_slice, 0)
    expect(15, s.slices_in)

    arrived(12)
    s.first_all[core, chip] = s.first_piece[0] + jnp.sum(s.first_z_in[...], axis=0)

    def spread(array, number):
        def step(k, c):
            start(array.at[core, chip], array.at[core, chip], number, (lax.rem(chip + k, chips) * 2 + core, z))
            return c
        lax.fori_loop(1, chips, step, 0)
        expect(number, array.at[0, pl.ds(0, chips - 1)])
    spread(s.first_all, 16)

    arrived(6)
    term = s.term[me] + jnp.sum(s.term_in[...], axis=0)
    arrived(15)
    mixed = s.slices[z] + jnp.sum(s.slices_in[...], axis=0)
    s.second_all[me] = (term - mixed) * scale

    def send_second(k, c):
        start(s.second_all.at[me], s.second_all.at[me], 17, (lax.rem(me + k, n_row), z))
        return c
    lax.fori_loop(1, n_row, send_second, 0)
    expect(17, s.second_all.at[pl.ds(0, n_row - 1)])

    arrived(16)
    start(s.first_all.at[core], s.first_all.at[core], 18, sibling)
    expect(18, s.first_all.at[0])
    arrived(18)
    out_first[...] = s.first_all[...]
    arrived(17)
    out_second[...] = s.second_all[...]
    finish()


def place(geometry, first, second, out_first, out_second, wide):
    ny, nx, nz = geometry
    half, piece = out_first.shape[1] // 2, first.shape[2]
    quarter = half // 2
    for y in range(ny):
        for x in range(nx):
            chip = y * nx + x
            for c in range(2):
                out_first[chip * piece:(chip + 1) * piece, c * half:(c + 1) * half] = first[c, chip]
                upper = c * half + x * (quarter // nx) + y * 8
                lower = c * half + quarter + y * (quarter // ny) + x * 8
                v = second[2 * chip + c]
                wide[upper:upper + 8, :] = v
                wide[lower:lower + 8, :] = pltpu.roll(v, 64, axis=1)
    for k in range(wide.shape[0] // LANES):
        out_second[:, k * LANES:(k + 1) * LANES] = jnp.transpose(wide[k * LANES:(k + 1) * LANES, :])[0:64, :]


def shards(geometry, noise, w_first, w_second, history):
    ny, nx, nz = geometry
    chips = ny * nx
    n_row = 2 * chips
    gen, zdim = noise.shape
    hist, width = history.shape
    hid = w_first.shape[1]
    half, quarter = hid // 2, hid // 4
    piece = zdim // chips
    jr, ir = hist // LANES, gen // LANES
    shapes = dict(
        hidden=((gen, hid), BF16), hidden_t=((hid, gen), BF16), noise_t=((zdim, gen), BF16),
        surface=((gen, width), BF16), mult=((gen, hid), F32), surf_w=((gen, hid), F32),
        hist_w_hi=((hist, hid), BF16), hist_w_lo=((hist, hid), BF16),
        plan=((gen, hist), F32), weights=((gen, hist), BF16),
        surf_sq=((gen, LANES), F32), hist_sq=((1, hist), F32),
        row_a=((gen, LANES), F32), row_b=((gen, LANES), F32), col_b=((jr, LANES), F32),
        m_pair=((2, jr, LANES), F32), m_pair_in=((n_row - 1, 2, jr, LANES), F32),
        m_col0=((2, ir, LANES), F32), m_col0_in=((nz - 1, 2, ir, LANES), F32),
        m_row=((SWEEPS, jr, LANES), F32), m_row_in=((SWEEPS - 1, n_row - 1, jr, LANES), F32),
        m_col=((SWEEPS - 1, ir, LANES), F32), m_col_in=((SWEEPS - 1, nz - 1, ir, LANES), F32),
        acc=((hid, hist), F32), acc_in=((half, hist), F32),
        x_in=((nx - 1, quarter // nx, hist), F32), y_in=((ny - 1, quarter // ny, hist), F32),
        x_in2=((nx - 1, 8, hist), F32), y_in2=((ny - 1, 8, hist), F32), reduced=((16, hist), F32),
        first=((zdim, hid), F32), first_in=((zdim, half), F32), first_half=((zdim, half), F32),
        first_chip_in=((chips - 1, piece, half), F32), first_piece=((1, piece, half), F32),
        first_z_in=((nz - 1, piece, half), F32), first_all=((2, chips, piece, half), F32),
        term_a=((hid, LANES), F32), term_b=((hid, LANES), F32),
        term=((n_row, 8, LANES), F32), term_in=((n_row - 1, 8, LANES), F32),
        mix=((16, width), F32), slices=((nz, 8, LANES), F32), slices_in=((nz - 1, 8, LANES), F32),
        second_all=((n_row, 8, LANES), F32),
    )
    scratch = [pltpu.VMEM(*shape) for shape in shapes.values()] + [pltpu.SemaphoreType.DMA((56,))]
    vmem = pl.BlockSpec(memory_space=pltpu.VMEM)
    first, second = pl.pallas_call(
        functools.partial(kernel, geometry, tuple(shapes)),
        out_shape=(
            jax.ShapeDtypeStruct((2, chips, piece, half), F32),
            jax.ShapeDtypeStruct((n_row, 8, LANES), F32),
        ),
        in_specs=[vmem] * 4,
        out_specs=(vmem, vmem),
        scratch_shapes=scratch,
        compiler_params=pltpu.CompilerParams(
            collective_id=0, has_side_effects=True, vmem_limit_bytes=56 * 1024 * 1024
        ),
        name="transport",
    )(noise, w_first, w_second, history)
    grad_first, turned = pl.pallas_call(
        functools.partial(place, geometry),
        out_shape=(
            jax.ShapeDtypeStruct((zdim, hid), F32),
            jax.ShapeDtypeStruct((width // nz, hid), F32),
        ),
        in_specs=[vmem] * 2,
        out_specs=(vmem, vmem),
        scratch_shapes=[pltpu.VMEM((hid, LANES), F32)],
        name="place",
    )(first, second)
    return grad_first, turned.T


def solution(mesh):
    chips = mesh.shape["row"] // 2
    nx = math.isqrt(chips)
    geometry = (chips // nx, nx, mesh.shape["col"])
    placed = (P("row", None), P(), P(), P("col", None))
    return jax.shard_map(
        functools.partial(shards, geometry), mesh=mesh, in_specs=placed,
        out_specs=(P(), P(None, "col")), check_vma=False,
    )
```

time: 106 us -> 97.4 us (0.919)
  Pallas kernels: 102 us -> 96.6 us
  local copies, waits for them, and re-layouts: 3.39 us -> 0 us
    pallas_call x1, Pallas kernels: 102 us -> 94.8 us  [shards(): pl.pallas_call(functools.partial(kernel, geometry, tuple(shapes)), out_sh...]
    pallas_call x0 -> x1, Pallas kernels: none -> 1.85 us  [shards(): pl.pallas_call(functools.partial(place, geometry), out_shape=(jax.ShapeDt...]
    pallas_call x1 -> x0, local copies, waits for them, and re-layouts: 1.72 us -> none  [shards(): pl.pallas_call(functools.partial(kernel, geometry, tuple(shapes)), out_sh...]
    unnamed x1 -> x0, local copies, waits for them, and re-layouts: 1.67 us -> none
where the time goes in v2:
time: 97.4 us; the launch traced here: 97.3 us
  Pallas kernels  96.6 us (99%)
    pallas_call x1, Pallas kernels, shards(): pl.pallas_call(functools.partial(kernel, geometry, tuple(shapes)), out_sh...  94.8 us

profile of v2, /device:TPU:1, one launch (start us, length us, event | category | flops | bytes accessed | tf_op | source)
XLA Modules:
  0.0 97.3 jit_solution(14617281485188989916)
XLA Ops:
  0.6 94.8 %transport.1 = (f32[2,16,8,256]{3,2,1,0:T(8,128)}, f32[32,8,128]{2,1,0:T(8,128)}) custom-call(bf16[512,128]{1,0:T(8,128)(2,1)} %noise.1, bf16[128,512]{1,0:T(8,128)(2,1)} %w_first.1, bf16[512,1024]{1,0:T(8,128)(2,1)} %w_second.1, bf16[1024,1024]{1,0:T(8,128)(2,1)} %history.1), custom_call_target="tpu_custom_call" | custom-call | tf_op jit(solution)/shard_map/transport/pallas_call | solution.py:506
  95.4 1.9 %place.1 = (f32[128,512]{1,0:T(8,128)}, f32[64,512]{1,0:T(8,128)}) custom-call(f32[2,16,8,256]{3,2,1,0:T(8,128)} %get-tuple-element.6.first, f32[32,8,128]{2,1,0:T(8,128)} %get-tuple-element.7.second), custom_call_target="tpu_custom_call" | custom-call | tf_op jit(solution)/shard_map/place/pallas_call | solution.py:520

commit v3 on v2

--- a/solution.py
+++ b/solution.py
@@ -17,12 +17,17 @@
 LANES = 128
 
 
-def kernel(geometry, names, noise, w_first, w_second, history, out_first, out_second, *scratch):
+def kernel(geometry, names, noise, w_first, w_second_hbm, history_hbm, out_first, out_second, *scratch):
     ny, nx, nz = geometry
     chips = ny * nx
     n_row, n_col = 2 * chips, nz
     s = SimpleNamespace(**dict(zip(names, scratch)))
     sem = scratch[-1]
+    w_second, history = s.w_second, s.history
+    load_w = pltpu.make_async_copy(w_second_hbm, w_second, sem.at[78])
+    load_h = pltpu.make_async_copy(history_hbm, history, sem.at[79])
+    load_w.start()
+    load_h.start()
     gen, zdim = noise.shape
     hist, width = history.shape
     hid = w_first.shape[1]
@@ -42,16 +47,32 @@
 
     barrier = pltpu.get_barrier_semaphore()
 
-    def greet_row(k, c):
-        pl.semaphore_signal(barrier, inc=1, device_id=(lax.rem(me + k, n_row), z), device_id_type=MESH)
-        return c
-
-    def greet_col(k, c):
-        pl.semaphore_signal(barrier, inc=1, device_id=(me, lax.rem(z + k, n_col)), device_id_type=MESH)
-        return c
-
-    lax.fori_loop(1, n_row, greet_row, 0)
-    lax.fori_loop(1, n_col, greet_col, 0)
+    def far(a, n):
+        return lax.rem(n // 2 + n * n - a * (a + 1) // 2, n)
+
+    def over_chips(send):
+        def step(j, c):
+            to_y, to_x = lax.rem(y + far(j // nx, ny), ny), lax.rem(x + far(lax.rem(j, nx), nx), nx)
+            send(to_y * nx + to_x, j)
+            return c
+        lax.fori_loop(0, chips - 1, step, 0)
+
+    def over_row(send):
+        def step(j, c):
+            k = j // 2
+            to_y, to_x = lax.rem(y + far(k // nx, ny), ny), lax.rem(x + far(lax.rem(k, nx), nx), nx)
+            send((to_y * nx + to_x) * 2 + lax.rem(core + 1 + j, 2), j)
+            return c
+        lax.fori_loop(0, n_row - 1, step, 0)
+
+    def over_col(send):
+        def step(j, c):
+            send(lax.rem(z + n_col // 2 + (j + 1) // 2 * (1 - 2 * lax.rem(j, 2)), n_col), j)
+            return c
+        lax.fori_loop(0, n_col - 1, step, 0)
+
+    over_col(lambda to, j: pl.semaphore_signal(barrier, inc=1, device_id=(me, to), device_id_type=MESH))
+    over_row(lambda to, j: pl.semaphore_signal(barrier, inc=1, device_id=(to, z), device_id_type=MESH))
 
     def start(src, dst, number, device):
         pltpu.make_async_remote_copy(
@@ -78,17 +99,11 @@
             wait_bytes(like, 2 * number)
 
     def to_row(src, dst, number):
-        def step(k, c):
-            start(src, dst.at[k - 1], number, (lax.rem(me + k, n_row), z))
-            return c
-        lax.fori_loop(1, n_row, step, 0)
+        over_row(lambda to, j: start(src, dst.at[j], number, (to, z)))
         expect(number, dst)
 
     def to_col(src, dst, number):
-        def step(k, c):
-            start(src, dst.at[k - 1], number, (me, lax.rem(z + k, n_col)))
-            return c
-        lax.fori_loop(1, n_col, step, 0)
+        over_col(lambda to, j: start(src, dst.at[j], number, (me, to)))
         expect(number, dst)
 
     def at(offset, size, unit):
@@ -131,6 +146,8 @@
         preact = dot(noise[...], w_first[:, cols])
         s.mult[:, cols] = preact
         s.hidden[:, cols] = (preact / (1.0 + jnp.exp(-preact))).astype(BF16)
+
+    load_w.wait()
 
     def surface_tile(n):
         cols = at(n * tile_g, tile_g, tile_g)
@@ -149,9 +166,7 @@
     each(blocks, surf_squares)
     s.surf_sq[...] = jnp.broadcast_to(jnp.sum(s.surf_sq[...], axis=1, keepdims=True), (gen, LANES))
 
-    def hist_squares(k):
-        s.hist_sq[:, block(k)] = jnp.sum(jnp.transpose(squares(history, block(k))), axis=0, keepdims=True)
-    each(hist // LANES, hist_squares)
+    load_h.wait()
 
     def inner_tile(n):
         cols = at(n * tile_j, tile_j, tile_j)
@@ -162,7 +177,7 @@
         rows, out = block(k), []
         own = s.surf_sq[rows, :]
         for cols, top in zip(plan_tiles, tops):
-            cost = (own + s.hist_sq[:, cols] - 2.0 * s.plan[rows, cols]) * (1.0 / width)
+            cost = (own - 2.0 * s.plan[rows, cols]) * (1.0 / width)
             scores = cost * (-1.0 / EPSILON)
             s.plan[rows, cols] = scores
             out.append(jnp.maximum(top, jnp.max(scores.reshape(LANES // 8, 8, LANES), axis=0)))
@@ -191,12 +206,18 @@
         s.hist_w_lo[rows, :] = (prod - hi.astype(F32)).astype(BF16)
     each(hist // min(256, hist), hist_w_tile)
 
+    def hist_squares(k):
+        s.hist_sq[pl.ds(k, 1), :] = jnp.sum(jnp.transpose(squares(history, block(k))), axis=0, keepdims=True)
+    each(hist // LANES, hist_squares)
+    hist_cost = s.hist_sq[...] * (1.0 / width) * (1.0 / EPSILON)
+
     arrived(0)
     tops, sums = s.m_pair_in[:, 0], s.m_pair_in[:, 1]
     top = jnp.maximum(jnp.max(tops, axis=0), s.m_pair[0])
     total = jnp.sum(sums * jnp.exp(tops - top[None]), axis=0)
     total = total + s.m_pair[1] * jnp.exp(s.m_pair[0] - top)
-    s.m_row[0] = math.log(gen_total) - (top + jnp.log(total))
+    g_first = math.log(gen_total) - (top + jnp.log(total) - hist_cost)
+    s.m_row[0] = g_first - hist_cost
 
     def row_tops(k):
         rows = block(k)
@@ -235,16 +256,12 @@
 
     def owner_term(o):
         oc, ox, oy = lax.rem(o, 2), lax.rem(o // 2, nx), o // (2 * nx)
-        upper = oc * half + ox * (quarter // nx) + oy * 8
-        lower = oc * half + quarter + oy * (quarter // ny) + ox * 8
+        upper = oc * half + oy * (quarter // ny) + ox * 8
+        lower = oc * half + quarter + ox * (quarter // nx) + oy * 8
         s.term[o] = jnp.where(low, s.term_a[at(upper, 8, 8), :], s.term_b[at(lower, 8, 8), :])
     each(n_row, owner_term)
 
-    def send_term(k, c):
-        peer = lax.rem(me + k, n_row)
-        start(s.term.at[peer], s.term_in.at[k - 1], 6, (peer, z))
-        return c
-    lax.fori_loop(1, n_row, send_term, 0)
+    over_row(lambda to, j: start(s.term.at[to], s.term_in.at[j], 6, (to, z)))
     expect(6, s.term_in)
 
     arrived(1)
@@ -318,13 +335,18 @@
     order = [pair for k in range(1, nx) for pair in ((True, k), (False, k))] + [(True, 0), (False, 0)]
 
     def block_rows(upper, k):
-        return lax.rem(x + k, nx) * span_x if upper else quarter + lax.rem(y + k, ny) * span_y
+        return lax.rem(y + k, ny) * span_y if upper else quarter + lax.rem(x + k, nx) * span_x
 
     for n, (upper, k) in enumerate(order):
         rows = block_rows(upper, k)
         start(s.acc.at[at(other * half + rows, span_x, 8), :], s.acc_in.at[at(rows, span_x, 8), :], 20 + n, sibling)
         expect(20 + n, s.acc_in.at[at(n * span_x, span_x, 8), :])
     acc_tile(core)
+
+    def chip_at(upper, k, first):
+        if upper == first:
+            return (y * nx + lax.rem(x + k, nx)) * 2 + core, lax.rem(x + k, nx) * 8
+        return (lax.rem(y + k, ny) * nx + x) * 2 + core, lax.rem(y + k, ny) * 8
 
     def pass_on(n):
         upper, k = order[n]
@@ -332,10 +354,22 @@
         arrived(20 + n)
         mine = at(core * half + rows, span_x, 8)
         s.acc[mine, :] = s.acc[mine, :] + s.acc_in[at(rows, span_x, 8), :]
-        if k and upper:
-            start(s.acc.at[mine, :], s.x_in.at[k - 1], 9, ((y * nx + lax.rem(x + k, nx)) * 2 + core, z))
-        elif k:
-            start(s.acc.at[mine, :], s.y_in.at[k - 1], 10, ((lax.rem(y + k, ny) * nx + x) * 2 + core, z))
+        into = s.x_in if upper else s.y_in
+        for j in range(1, nx):
+            device, offset = chip_at(upper, j, True)
+            start(s.acc.at[at(core * half + rows + offset, 8, 8), :], into.at[k, j - 1], 30 + n, (device, z))
+        expect(30 + n, into.at[k])
+
+    def pass_second(n):
+        upper, k = order[n]
+        arrived(30 + n)
+        rows = at(core * half + block_rows(upper, k) + chip_at(upper, 0, True)[1], 8, 8)
+        total = s.acc[rows, :] + jnp.sum((s.x_in if upper else s.y_in)[k], axis=0)
+        if k == 0:
+            return total
+        s.acc[rows, :] = total
+        into = s.y_in2 if upper else s.x_in2
+        start(s.acc.at[rows, :], into.at[k - 1], 13 if upper else 14, (chip_at(upper, k, False)[0], z))
 
     def first_tile(n):
         cols = at(n * tile_h, tile_h, tile_h)
@@ -347,51 +381,32 @@
         s.first[:, cols] = dot(s.noise_t[...], hi) + dot(s.noise_t[...], lo)
 
     for n in range(2):
-        pass_on(2 * n)
-        pass_on(2 * n + 1)
+        for k in range(4):
+            pass_on(4 * n + k)
         first_tile(n)
     start(s.first.at[:, at(other * half, half, half)], s.first_in, 8, sibling)
     expect(8, s.first_in)
-    for n in range(4, len(order)):
-        pass_on(n)
-    expect(9, s.x_in)
-    expect(10, s.y_in)
+    pass_second(0)
+    pass_second(1)
 
     arrived(8)
     s.first_half[...] = s.first[:, at(core * half, half, half)] + s.first_in[...]
     piece = zdim // chips
-
-    def send_first(k, c):
-        to = lax.rem(chip + k, chips)
-        start(s.first_half.at[at(to * piece, piece, 8), :], s.first_chip_in.at[k - 1], 11,
-              (to * 2 + core, z))
-        return c
-    lax.fori_loop(1, chips, send_first, 0)
+    over_chips(lambda to, j: start(
+        s.first_half.at[at(to * piece, piece, 8), :], s.first_chip_in.at[j], 11, (to * 2 + core, z)))
     expect(11, s.first_chip_in)
+    for n in range(2, len(order) - 2):
+        pass_second(n)
+    expect(13, s.y_in2)
+    expect(14, s.x_in2)
+    own_u, own_l = pass_second(len(order) - 2), pass_second(len(order) - 1)
     arrived(11)
     s.first_piece[0] = s.first_half[at(chip * piece, piece, 8), :] + jnp.sum(s.first_chip_in[...], axis=0)
     to_col(s.first_piece.at[0], s.first_z_in, 12)
-
-    arrived(9)
-    arrived(10)
-    rows_u, rows_l = at(base_u + x * span_x, span_x, 8), at(base_l + y * span_y, span_y, 8)
-    s.acc[rows_u, :] = s.acc[rows_u, :] + jnp.sum(s.x_in[...], axis=0)
-    s.acc[rows_l, :] = s.acc[rows_l, :] + jnp.sum(s.y_in[...], axis=0)
-    for k in range(1, ny):
-        to = lax.rem(y + k, ny)
-        start(s.acc.at[at(base_u + x * span_x + to * 8, 8, 8), :], s.y_in2.at[k - 1], 13,
-              ((to * nx + x) * 2 + core, z))
-    for k in range(1, nx):
-        to = lax.rem(x + k, nx)
-        start(s.acc.at[at(base_l + y * span_y + to * 8, 8, 8), :], s.x_in2.at[k - 1], 14,
-              ((y * nx + to) * 2 + core, z))
-    expect(13, s.y_in2)
-    expect(14, s.x_in2)
     arrived(13)
     arrived(14)
-    mine_u, mine_l = base_u + x * span_x + y * 8, base_l + y * span_y + x * 8
-    s.reduced[0:8, :] = s.acc[at(mine_u, 8, 8), :] + jnp.sum(s.y_in2[...], axis=0)
-    s.reduced[8:16, :] = s.acc[at(mine_l, 8, 8), :] + jnp.sum(s.x_in2[...], axis=0)
+    s.reduced[0:8, :] = own_u + jnp.sum(s.y_in2[...], axis=0)
+    s.reduced[8:16, :] = own_l + jnp.sum(s.x_in2[...], axis=0)
 
     hi = s.reduced[...].astype(BF16)
     lo = (s.reduced[...] - hi.astype(F32)).astype(BF16)
@@ -411,23 +426,15 @@
         else:
             s.slices[k] = jnp.where(low, pltpu.roll(upper, 64, axis=1), lower)
 
-    def send_slice(k, c):
-        to = lax.rem(z + k, n_col)
-        start(s.slices.at[to], s.slices_in.at[k - 1], 15, (me, to))
-        return c
-    lax.fori_loop(1, n_col, send_slice, 0)
+    over_col(lambda to, j: start(s.slices.at[to], s.slices_in.at[j], 15, (me, to)))
     expect(15, s.slices_in)
 
     arrived(12)
     s.first_all[core, chip] = s.first_piece[0] + jnp.sum(s.first_z_in[...], axis=0)
 
-    def spread(array, number):
-        def step(k, c):
-            start(array.at[core, chip], array.at[core, chip], number, (lax.rem(chip + k, chips) * 2 + core, z))
-            return c
-        lax.fori_loop(1, chips, step, 0)
-        expect(number, array.at[0, pl.ds(0, chips - 1)])
-    spread(s.first_all, 16)
+    over_chips(lambda to, j: start(
+        s.first_all.at[core, chip], s.first_all.at[core, chip], 16, (to * 2 + core, z)))
+    expect(16, s.first_all.at[0, pl.ds(0, chips - 1)])
 
     arrived(6)
     term = s.term[me] + jnp.sum(s.term_in[...], axis=0)
@@ -435,10 +442,7 @@
     mixed = s.slices[z] + jnp.sum(s.slices_in[...], axis=0)
     s.second_all[me] = (term - mixed) * scale
 
-    def send_second(k, c):
-        start(s.second_all.at[me], s.second_all.at[me], 17, (lax.rem(me + k, n_row), z))
-        return c
-    lax.fori_loop(1, n_row, send_second, 0)
+    over_row(lambda to, j: start(s.second_all.at[me], s.second_all.at[me], 17, (to, z)))
     expect(17, s.second_all.at[pl.ds(0, n_row - 1)])
 
     arrived(16)
@@ -460,8 +464,8 @@
             chip = y * nx + x
             for c in range(2):
                 out_first[chip * piece:(chip + 1) * piece, c * half:(c + 1) * half] = first[c, chip]
-                upper = c * half + x * (quarter // nx) + y * 8
-                lower = c * half + quarter + y * (quarter // ny) + x * 8
+                upper = c * half + y * (quarter // ny) + x * 8
+                lower = c * half + quarter + x * (quarter // nx) + y * 8
                 v = second[2 * chip + c]
                 wide[upper:upper + 8, :] = v
                 wide[lower:lower + 8, :] = pltpu.roll(v, 64, axis=1)
@@ -480,18 +484,19 @@
     piece = zdim // chips
     jr, ir = hist // LANES, gen // LANES
     shapes = dict(
+        w_second=((hid, width), BF16), history=((hist, width), BF16),
         hidden=((gen, hid), BF16), hidden_t=((hid, gen), BF16), noise_t=((zdim, gen), BF16),
         surface=((gen, width), BF16), mult=((gen, hid), F32), surf_w=((gen, hid), F32),
         hist_w_hi=((hist, hid), BF16), hist_w_lo=((hist, hid), BF16),
         plan=((gen, hist), F32), weights=((gen, hist), BF16),
-        surf_sq=((gen, LANES), F32), hist_sq=((1, hist), F32),
+        surf_sq=((gen, LANES), F32), hist_sq=((jr, LANES), F32),
         row_a=((gen, LANES), F32), row_b=((gen, LANES), F32), col_b=((jr, LANES), F32),
         m_pair=((2, jr, LANES), F32), m_pair_in=((n_row - 1, 2, jr, LANES), F32),
         m_col0=((2, ir, LANES), F32), m_col0_in=((nz - 1, 2, ir, LANES), F32),
         m_row=((SWEEPS, jr, LANES), F32), m_row_in=((SWEEPS - 1, n_row - 1, jr, LANES), F32),
         m_col=((SWEEPS - 1, ir, LANES), F32), m_col_in=((SWEEPS - 1, nz - 1, ir, LANES), F32),
         acc=((hid, hist), F32), acc_in=((half, hist), F32),
-        x_in=((nx - 1, quarter // nx, hist), F32), y_in=((ny - 1, quarter // ny, hist), F32),
+        x_in=((ny, nx - 1, 8, hist), F32), y_in=((nx, ny - 1, 8, hist), F32),
         x_in2=((nx - 1, 8, hist), F32), y_in2=((ny - 1, 8, hist), F32), reduced=((16, hist), F32),
         first=((zdim, hid), F32), first_in=((zdim, half), F32), first_half=((zdim, half), F32),
         first_chip_in=((chips - 1, piece, half), F32), first_piece=((1, piece, half), F32),
@@ -501,7 +506,7 @@
         mix=((16, width), F32), slices=((nz, 8, LANES), F32), slices_in=((nz - 1, 8, LANES), F32),
         second_all=((n_row, 8, LANES), F32),
     )
-    scratch = [pltpu.VMEM(*shape) for shape in shapes.values()] + [pltpu.SemaphoreType.DMA((56,))]
+    scratch = [pltpu.VMEM(*shape) for shape in shapes.values()] + [pltpu.SemaphoreType.DMA((80,))]
     vmem = pl.BlockSpec(memory_space=pltpu.VMEM)
     first, second = pl.pallas_call(
         functools.partial(kernel, geometry, tuple(shapes)),
@@ -509,7 +514,7 @@
             jax.ShapeDtypeStruct((2, chips, piece, half), F32),
             jax.ShapeDtypeStruct((n_row, 8, LANES), F32),
         ),
-        in_specs=[vmem] * 4,
+        in_specs=[vmem] * 2 + [pl.BlockSpec(memory_space=pl.ANY)] * 2,
         out_specs=(vmem, vmem),
         scratch_shapes=scratch,
         compiler_params=pltpu.CompilerParams(

time: 97.4 us -> 92.9 us (0.954)
  Pallas kernels: 96.6 us -> 92.1 us
    pallas_call x1, Pallas kernels: 94.8 us -> 90.2 us  [shards(): pl.pallas_call(functools.partial(kernel, geometry, tuple(shapes)), out_sh...]
where the time goes in v3:
time: 92.9 us; the launch traced here: 92.7 us
  Pallas kernels  92.1 us (99%)
    pallas_call x1, Pallas kernels, shards(): pl.pallas_call(functools.partial(kernel, geometry, tuple(shapes)), out_sh...  90.2 us
    pallas_call x1, Pallas kernels, shards(): pl.pallas_call(functools.partial(place, geometry), out_shape=(jax.ShapeDt...  1.87 us

profile of v3, /device:TPU:1, one launch (start us, length us, event | category | flops | bytes accessed | tf_op | source)
XLA Modules:
  0.0 92.7 jit_solution(12902450145951440274)
XLA Ops:
  0.6 90.2 %transport.1 = (f32[2,16,8,256]{3,2,1,0:T(8,128)}, f32[32,8,128]{2,1,0:T(8,128)}) custom-call(bf16[512,128]{1,0:T(8,128)(2,1)} %noise.1, bf16[128,512]{1,0:T(8,128)(2,1)} %w_first.1, bf16[512,1024]{1,0:T(8,128)(2,1)} %w_second_hbm.1, bf16[1024,1024]{1,0:T(8,128)(2,1)} %history_hbm.1), custom_call_target="tpu_custom_call" | custom-call | tf_op jit(solution)/shard_map/transport/pallas_call | solution.py:511
  90.8 1.9 %place.1 = (f32[128,512]{1,0:T(8,128)}, f32[64,512]{1,0:T(8,128)}) custom-call(f32[2,16,8,256]{3,2,1,0:T(8,128)} %get-tuple-element.6.first, f32[32,8,128]{2,1,0:T(8,128)} %get-tuple-element.7.second), custom_call_target="tpu_custom_call" | custom-call | tf_op jit(solution)/shard_map/place/pallas_call | solution.py:525

commit v4 on v3

--- a/solution.py
+++ b/solution.py
@@ -122,6 +122,13 @@
     def fold(v):
         return jnp.sum(v.reshape(LANES // 8, 8, LANES), axis=0)
 
+    def squares(ref, rows, across):
+        total = jnp.zeros((LANES, LANES), F32)
+        for cols in across:
+            v = ref[rows, cols].astype(F32)
+            total = total + v * v
+        return total
+
     def rows_from_column(column, dst, total):
         for k in range(dst.shape[0]):
             turned = jnp.transpose(column[tiles[k], :])
@@ -149,54 +156,34 @@
 
     load_w.wait()
 
-    def surface_tile(n):
-        cols = at(n * tile_g, tile_g, tile_g)
+    for n in range(width // tile_g):
+        cols = slice(n * tile_g, (n + 1) * tile_g)
         s.surface[:, cols] = dot(s.hidden[...], w_second[:, cols]).astype(BF16)
-    each(width // tile_g, surface_tile)
-
-    def squares(ref, rows):
-        total = jnp.zeros((LANES, LANES), F32)
-        for cols in tiles[:width // LANES]:
-            v = ref[rows, cols].astype(F32)
-            total = total + v * v
-        return total
-
-    def surf_squares(k):
-        s.surf_sq[block(k), :] = squares(s.surface, block(k))
-    each(blocks, surf_squares)
+        for k in range(blocks):
+            total = squares(s.surface, tiles[k], tiles[n * tile_g // LANES:(n + 1) * tile_g // LANES])
+            s.surf_sq[tiles[k], :] = total if n == 0 else s.surf_sq[tiles[k], :] + total
     s.surf_sq[...] = jnp.broadcast_to(jnp.sum(s.surf_sq[...], axis=1, keepdims=True), (gen, LANES))
 
     load_h.wait()
-
-    def inner_tile(n):
-        cols = at(n * tile_j, tile_j, tile_j)
-        s.plan[:, cols] = dot_t(s.surface[...], history[cols, :])
-    each(hist // tile_j, inner_tile)
-
-    def score_block(k, tops):
-        rows, out = block(k), []
-        own = s.surf_sq[rows, :]
-        for cols, top in zip(plan_tiles, tops):
-            cost = (own - 2.0 * s.plan[rows, cols]) * (1.0 / width)
-            scores = cost * (-1.0 / EPSILON)
-            s.plan[rows, cols] = scores
-            out.append(jnp.maximum(top, jnp.max(scores.reshape(LANES // 8, 8, LANES), axis=0)))
-        return tuple(out)
-    tops = lax.fori_loop(0, blocks, score_block, tuple(jnp.full((8, LANES), -jnp.inf, F32) for _ in plan_tiles))
-    for k, top in enumerate(tops):
-        s.m_pair[0, k:k + 1, :] = jnp.max(top, axis=0, keepdims=True)
-
-    def score_sums(k, sums):
-        rows, out = block(k), []
-        for n, (cols, total) in enumerate(zip(plan_tiles, sums)):
-            out.append(total + fold(jnp.exp(s.plan[rows, cols] - s.m_pair[0, n:n + 1, :])))
-        return tuple(out)
-    zeros = tuple(jnp.zeros((8, LANES), F32) for _ in plan_tiles)
-    for k, total in enumerate(lax.fori_loop(0, blocks, score_sums, zeros)):
-        s.m_pair[1, k:k + 1, :] = jnp.sum(total, axis=0, keepdims=True)
+    for n in range(hist // tile_j):
+        wide = slice(n * tile_j, (n + 1) * tile_j)
+        s.plan[:, wide] = dot_t(s.surface[...], history[wide, :])
+        for c in range(n * tile_j // LANES, (n + 1) * tile_j // LANES):
+            top = None
+            for k in range(blocks):
+                cost = (s.surf_sq[tiles[k], :] - 2.0 * s.plan[tiles[k], tiles[c]]) * (1.0 / width)
+                scores = cost * (-1.0 / EPSILON)
+                s.plan[tiles[k], tiles[c]] = scores
+                tall = jnp.max(scores.reshape(LANES // 8, 8, LANES), axis=0)
+                top = tall if top is None else jnp.maximum(top, tall)
+            top = jnp.max(top, axis=0, keepdims=True)
+            total = jnp.zeros((8, LANES), F32)
+            for k in range(blocks):
+                total = total + fold(jnp.exp(s.plan[tiles[k], tiles[c]] - top))
+            s.m_lse[c:c + 1, :] = top + jnp.log(jnp.sum(total, axis=0, keepdims=True))
 
     pl.semaphore_wait(barrier, n_row - 1 + n_col - 1)
-    to_row(s.m_pair, s.m_pair_in, 0)
+    to_row(s.m_lse, s.m_lse_in, 0)
 
     def hist_w_tile(n):
         rows = at(n * 256, min(256, hist), min(256, hist))
@@ -207,15 +194,14 @@
     each(hist // min(256, hist), hist_w_tile)
 
     def hist_squares(k):
-        s.hist_sq[pl.ds(k, 1), :] = jnp.sum(jnp.transpose(squares(history, block(k))), axis=0, keepdims=True)
+        s.hist_sq[pl.ds(k, 1), :] = jnp.sum(
+            jnp.transpose(squares(history, block(k), tiles[:width // LANES])), axis=0, keepdims=True)
     each(hist // LANES, hist_squares)
     hist_cost = s.hist_sq[...] * (1.0 / width) * (1.0 / EPSILON)
 
     arrived(0)
-    tops, sums = s.m_pair_in[:, 0], s.m_pair_in[:, 1]
-    top = jnp.maximum(jnp.max(tops, axis=0), s.m_pair[0])
-    total = jnp.sum(sums * jnp.exp(tops - top[None]), axis=0)
-    total = total + s.m_pair[1] * jnp.exp(s.m_pair[0] - top)
+    top = jnp.maximum(jnp.max(s.m_lse_in[...], axis=0), s.m_lse[...])
+    total = jnp.sum(jnp.exp(s.m_lse_in[...] - top[None]), axis=0) + jnp.exp(s.m_lse[...] - top)
     g_first = math.log(gen_total) - (top + jnp.log(total) - hist_cost)
     s.m_row[0] = g_first - hist_cost
 
@@ -225,7 +211,8 @@
         for n, cols in enumerate(plan_tiles[1:], 1):
             top = jnp.maximum(top, s.plan[rows, cols] + s.m_row[0, n:n + 1, :])
         s.row_a[rows, :] = top
-    each(blocks, row_tops)
+    for k in range(blocks):
+        row_tops(k)
     s.row_a[...] = jnp.broadcast_to(jnp.max(s.row_a[...], axis=1, keepdims=True), (gen, LANES))
 
     def first_rows(k):
@@ -236,10 +223,12 @@
             s.plan[rows, cols] = grown
             total = total + grown
         s.row_b[rows, :] = total
-    each(blocks, first_rows)
-    rows_from_column(s.row_a, s.m_col0.at[0], False)
-    rows_from_column(s.row_b, s.m_col0.at[1], True)
-    to_col(s.m_col0, s.m_col0_in, 1)
+    for k in range(blocks):
+        first_rows(k)
+    rows_from_column(s.row_a, s.row_top, False)
+    rows_from_column(s.row_b, s.row_lse, True)
+    s.row_lse[...] = s.row_top[...] + jnp.log(s.row_lse[...])
+    to_col(s.row_lse, s.row_lse_in, 1)
 
     def surf_w_tile(n):
         cols = at(n * tile_h, tile_h, tile_h)
@@ -265,11 +254,9 @@
     expect(6, s.term_in)
 
     arrived(1)
-    tops, sums = s.m_col0_in[:, 0], s.m_col0_in[:, 1]
-    top = jnp.maximum(jnp.max(tops, axis=0), s.m_col0[0])
-    total = jnp.sum(sums * jnp.exp(tops - top[None]), axis=0)
-    total = total + s.m_col0[1] * jnp.exp(s.m_col0[0] - top)
-    column_from_rows(jnp.exp(s.m_col0[0] - top) / total, s.row_a)
+    top = jnp.maximum(jnp.max(s.row_lse_in[...], axis=0), s.row_lse[...])
+    total = jnp.sum(jnp.exp(s.row_lse_in[...] - top[None]), axis=0) + jnp.exp(s.row_lse[...] - top)
+    column_from_rows(jnp.exp(s.row_top[...] - top) / total, s.row_a)
 
     def column_sums(scaled, dst):
         def step(k, sums):
@@ -281,7 +268,10 @@
                     s.plan[rows, cols] = v
                 out.append(total + fold(v))
             return tuple(out)
-        for k, total in enumerate(lax.fori_loop(0, blocks, step, zeros)):
+        sums = [jnp.zeros((8, LANES), F32) for _ in plan_tiles]
+        for k in range(blocks):
+            sums = step(k, sums)
+        for k, total in enumerate(sums):
             dst[k:k + 1, :] = jnp.sum(total, axis=0, keepdims=True)
 
     def row_sums(k):
@@ -290,6 +280,19 @@
         for n, cols in enumerate(plan_tiles):
             total = total + s.plan[rows, cols] * s.col_b[n:n + 1, :]
         s.row_b[rows, :] = total
+
+    def unscaled_rows(k):
+        rows = block(k)
+        for n, cols in enumerate(plan_tiles):
+            v = s.plan[rows, cols] * s.col_b[n:n + 1, :]
+            hi = v.astype(BF16)
+            s.plan_hi[rows, cols] = hi
+            s.plan_lo[rows, cols] = (v - hi.astype(F32)).astype(BF16)
+
+    def value_tile(n):
+        cols = at(n * tile_h, tile_h, tile_h)
+        s.value[:, cols] = (dot(s.plan_hi[...], s.hist_w_hi[:, cols]) + dot(s.plan_hi[...], s.hist_w_lo[:, cols])
+                            + dot(s.plan_lo[...], s.hist_w_hi[:, cols]))
 
     for sweep in range(1, SWEEPS):
         number = 2 * sweep
@@ -305,10 +308,15 @@
         total = mine[...] + jnp.sum(theirs[...], axis=0)
         s.col_b[...] = (gen_total / hist_total) / total
 
-        each(blocks, row_sums)
+        for k in range(blocks):
+            row_sums(k)
         mine, theirs = s.m_col.at[sweep - 1], s.m_col_in.at[sweep - 1]
         rows_from_column(s.row_b, mine, True)
         to_col(mine, theirs, number + 1)
+        if sweep == SWEEPS - 1:
+            for k in range(blocks):
+                unscaled_rows(k)
+            each(hid // tile_h, value_tile)
         arrived(number + 1)
         total = mine[...] + jnp.sum(theirs[...], axis=0)
         column_from_rows(1.0 / total, s.row_a)
@@ -318,7 +326,8 @@
         own = s.row_a[rows, :]
         for n, cols in enumerate(plan_tiles):
             s.weights[rows, cols] = (s.plan[rows, cols] * own * s.col_b[n:n + 1, :]).astype(BF16)
-    each(blocks, weight_rows)
+    for k in range(blocks):
+        weight_rows(k)
 
     def acc_tile(which):
         rows = at(which * half, half, half)
@@ -341,7 +350,6 @@
         rows = block_rows(upper, k)
         start(s.acc.at[at(other * half + rows, span_x, 8), :], s.acc_in.at[at(rows, span_x, 8), :], 20 + n, sibling)
         expect(20 + n, s.acc_in.at[at(n * span_x, span_x, 8), :])
-    acc_tile(core)
 
     def chip_at(upper, k, first):
         if upper == first:
@@ -371,21 +379,21 @@
         into = s.y_in2 if upper else s.x_in2
         start(s.acc.at[rows, :], into.at[k - 1], 13 if upper else 14, (chip_at(upper, k, False)[0], z))
 
-    def first_tile(n):
-        cols = at(n * tile_h, tile_h, tile_h)
-        value = dot(s.weights[...], s.hist_w_hi[:, cols]) + dot(s.weights[...], s.hist_w_lo[:, cols])
-        d_hidden = (s.surf_w[:, cols] * (1.0 / n_col) - value) * scale
-        d_preact = d_hidden * s.mult[:, cols]
-        hi = d_preact.astype(BF16)
-        lo = (d_preact - hi.astype(F32)).astype(BF16)
-        s.first[:, cols] = dot(s.noise_t[...], hi) + dot(s.noise_t[...], lo)
-
-    for n in range(2):
-        for k in range(4):
-            pass_on(4 * n + k)
-        first_tile(n)
+    for k in range(blocks):
+        for cols in tiles[:hid // LANES]:
+            rows = tiles[k]
+            d_hidden = (s.surf_w[rows, cols] * (1.0 / n_col) - s.value[rows, cols] * s.row_a[rows, :]) * scale
+            d_preact = d_hidden * s.mult[rows, cols]
+            hi = d_preact.astype(BF16)
+            s.d_hi[rows, cols] = hi
+            s.d_lo[rows, cols] = (d_preact - hi.astype(F32)).astype(BF16)
+    s.first[...] = dot(s.noise_t[...], s.d_hi[...]) + dot(s.noise_t[...], s.d_lo[...])
     start(s.first.at[:, at(other * half, half, half)], s.first_in, 8, sibling)
     expect(8, s.first_in)
+    acc_tile(core)
+
+    for n in range(len(order)):
+        pass_on(n)
     pass_second(0)
     pass_second(1)
 
@@ -491,8 +499,10 @@
         plan=((gen, hist), F32), weights=((gen, hist), BF16),
         surf_sq=((gen, LANES), F32), hist_sq=((jr, LANES), F32),
         row_a=((gen, LANES), F32), row_b=((gen, LANES), F32), col_b=((jr, LANES), F32),
-        m_pair=((2, jr, LANES), F32), m_pair_in=((n_row - 1, 2, jr, LANES), F32),
-        m_col0=((2, ir, LANES), F32), m_col0_in=((nz - 1, 2, ir, LANES), F32),
+        m_lse=((jr, LANES), F32), m_lse_in=((n_row - 1, jr, LANES), F32),
+        row_top=((ir, LANES), F32), row_lse=((ir, LANES), F32), row_lse_in=((nz - 1, ir, LANES), F32),
+        plan_hi=((gen, hist), BF16), plan_lo=((gen, hist), BF16), value=((gen, hid), F32),
+        d_hi=((gen, hid), BF16), d_lo=((gen, hid), BF16),
         m_row=((SWEEPS, jr, LANES), F32), m_row_in=((SWEEPS - 1, n_row - 1, jr, LANES), F32),
         m_col=((SWEEPS - 1, ir, LANES), F32), m_col_in=((SWEEPS - 1, nz - 1, ir, LANES), F32),
         acc=((hid, hist), F32), acc_in=((half, hist), F32),

time: 92.9 us -> 91.5 us (0.985)
  Pallas kernels: 92.1 us -> 90.7 us
    pallas_call x1, Pallas kernels: 90.2 us -> 88.8 us  [shards(): pl.pallas_call(functools.partial(kernel, geometry, tuple(shapes)), out_sh...]
where the time goes in v4:
time: 91.5 us; the launch traced here: 91.3 us
  Pallas kernels  90.7 us (99%)
    pallas_call x1, Pallas kernels, shards(): pl.pallas_call(functools.partial(kernel, geometry, tuple(shapes)), out_sh...  88.8 us
    pallas_call x1, Pallas kernels, shards(): pl.pallas_call(functools.partial(place, geometry), out_shape=(jax.ShapeDt...  1.87 us

profile of v4, /device:TPU:1, one launch (start us, length us, event | category | flops | bytes accessed | tf_op | source)
XLA Modules:
  0.0 91.3 jit_solution(6000313984264224990)
XLA Ops:
  0.6 88.8 %transport.1 = (f32[2,16,8,256]{3,2,1,0:T(8,128)}, f32[32,8,128]{2,1,0:T(8,128)}) custom-call(bf16[512,128]{1,0:T(8,128)(2,1)} %noise.1, bf16[128,512]{1,0:T(8,128)(2,1)} %w_first.1, bf16[512,1024]{1,0:T(8,128)(2,1)} %w_second_hbm.1, bf16[1024,1024]{1,0:T(8,128)(2,1)} %history_hbm.1), custom_call_target="tpu_custom_call" | custom-call | tf_op jit(solution)/shard_map/transport/pallas_call | solution.py:521
  89.4 1.9 %place.1 = (f32[128,512]{1,0:T(8,128)}, f32[64,512]{1,0:T(8,128)}) custom-call(f32[2,16,8,256]{3,2,1,0:T(8,128)} %get-tuple-element.6.first, f32[32,8,128]{2,1,0:T(8,128)} %get-tuple-element.7.second), custom_call_target="tpu_custom_call" | custom-call | tf_op jit(solution)/shard_map/place/pallas_call | solution.py:535

commit v5 on v4

--- a/solution.py
+++ b/solution.py
@@ -394,8 +394,6 @@
 
     for n in range(len(order)):
         pass_on(n)
-    pass_second(0)
-    pass_second(1)
 
     arrived(8)
     s.first_half[...] = s.first[:, at(core * half, half, half)] + s.first_in[...]
@@ -403,14 +401,14 @@
     over_chips(lambda to, j: start(
         s.first_half.at[at(to * piece, piece, 8), :], s.first_chip_in.at[j], 11, (to * 2 + core, z)))
     expect(11, s.first_chip_in)
-    for n in range(2, len(order) - 2):
+    for n in range(len(order) - 2):
         pass_second(n)
     expect(13, s.y_in2)
     expect(14, s.x_in2)
-    own_u, own_l = pass_second(len(order) - 2), pass_second(len(order) - 1)
     arrived(11)
     s.first_piece[0] = s.first_half[at(chip * piece, piece, 8), :] + jnp.sum(s.first_chip_in[...], axis=0)
     to_col(s.first_piece.at[0], s.first_z_in, 12)
+    own_u, own_l = pass_second(len(order) - 2), pass_second(len(order) - 1)
     arrived(13)
     arrived(14)
     s.reduced[0:8, :] = own_u + jnp.sum(s.y_in2[...], axis=0)
@@ -420,29 +418,23 @@
     lo = (s.reduced[...] - hi.astype(F32)).astype(BF16)
     both = jnp.concatenate([hi, lo], axis=0)
 
-    def mix_tile(n):
-        cols = at(n * tile_g, tile_g, tile_g)
-        prod = dot(both, history[:, cols])
-        s.mix[:, cols] = prod[0:16] + prod[16:32]
-    each(width // tile_g, mix_tile)
     low = lax.broadcasted_iota(jnp.int32, (8, LANES), 1) < 64
-    for k in range(nz):
-        lanes = slice((k // 2) * LANES, (k // 2 + 1) * LANES)
-        upper, lower = s.mix[0:8, lanes], s.mix[8:16, lanes]
-        if k % 2 == 0:
+    for n in range(width // tile_g):
+        prod = dot(both, history[:, n * tile_g:(n + 1) * tile_g])
+        prod = prod[0:16] + prod[16:32]
+        for c in range(tile_g // LANES):
+            upper, lower = prod[0:8, tiles[c]], prod[8:16, tiles[c]]
+            k = 2 * (n * tile_g // LANES + c)
             s.slices[k] = jnp.where(low, upper, pltpu.roll(lower, 64, axis=1))
-        else:
-            s.slices[k] = jnp.where(low, pltpu.roll(upper, 64, axis=1), lower)
+            s.slices[k + 1] = jnp.where(low, pltpu.roll(upper, 64, axis=1), lower)
 
     over_col(lambda to, j: start(s.slices.at[to], s.slices_in.at[j], 15, (me, to)))
     expect(15, s.slices_in)
 
     arrived(12)
-    s.first_all[core, chip] = s.first_piece[0] + jnp.sum(s.first_z_in[...], axis=0)
-
-    over_chips(lambda to, j: start(
-        s.first_all.at[core, chip], s.first_all.at[core, chip], 16, (to * 2 + core, z)))
-    expect(16, s.first_all.at[0, pl.ds(0, chips - 1)])
+    s.first_all[me] = s.first_piece[0] + jnp.sum(s.first_z_in[...], axis=0)
+    over_row(lambda to, j: start(s.first_all.at[me], s.first_all.at[me], 16, (to, z)))
+    expect(16, s.first_all.at[pl.ds(0, n_row - 1)])
 
     arrived(6)
     term = s.term[me] + jnp.sum(s.term_in[...], axis=0)
@@ -454,9 +446,6 @@
     expect(17, s.second_all.at[pl.ds(0, n_row - 1)])
 
     arrived(16)
-    start(s.first_all.at[core], s.first_all.at[core], 18, sibling)
-    expect(18, s.first_all.at[0])
-    arrived(18)
     out_first[...] = s.first_all[...]
     arrived(17)
     out_second[...] = s.second_all[...]
@@ -465,13 +454,13 @@
 
 def place(geometry, first, second, out_first, out_second, wide):
     ny, nx, nz = geometry
-    half, piece = out_first.shape[1] // 2, first.shape[2]
+    half, piece = out_first.shape[1] // 2, first.shape[1]
     quarter = half // 2
     for y in range(ny):
         for x in range(nx):
             chip = y * nx + x
             for c in range(2):
-                out_first[chip * piece:(chip + 1) * piece, c * half:(c + 1) * half] = first[c, chip]
+                out_first[chip * piece:(chip + 1) * piece, c * half:(c + 1) * half] = first[2 * chip + c]
                 upper = c * half + y * (quarter // ny) + x * 8
                 lower = c * half + quarter + x * (quarter // nx) + y * 8
                 v = second[2 * chip + c]
@@ -510,10 +499,10 @@
         x_in2=((nx - 1, 8, hist), F32), y_in2=((ny - 1, 8, hist), F32), reduced=((16, hist), F32),
         first=((zdim, hid), F32), first_in=((zdim, half), F32), first_half=((zdim, half), F32),
         first_chip_in=((chips - 1, piece, half), F32), first_piece=((1, piece, half), F32),
-        first_z_in=((nz - 1, piece, half), F32), first_all=((2, chips, piece, half), F32),
+        first_z_in=((nz - 1, piece, half), F32), first_all=((n_row, piece, half), F32),
         term_a=((hid, LANES), F32), term_b=((hid, LANES), F32),
         term=((n_row, 8, LANES), F32), term_in=((n_row - 1, 8, LANES), F32),
-        mix=((16, width), F32), slices=((nz, 8, LANES), F32), slices_in=((nz - 1, 8, LANES), F32),
+        slices=((nz, 8, LANES), F32), slices_in=((nz - 1, 8, LANES), F32),
         second_all=((n_row, 8, LANES), F32),
     )
     scratch = [pltpu.VMEM(*shape) for shape in shapes.values()] + [pltpu.SemaphoreType.DMA((80,))]
@@ -521,7 +510,7 @@
     first, second = pl.pallas_call(
         functools.partial(kernel, geometry, tuple(shapes)),
         out_shape=(
-            jax.ShapeDtypeStruct((2, chips, piece, half), F32),
+            jax.ShapeDtypeStruct((n_row, piece, half), F32),
             jax.ShapeDtypeStruct((n_row, 8, LANES), F32),
         ),
         in_specs=[vmem] * 2 + [pl.BlockSpec(memory_space=pl.ANY)] * 2,

time: 91.5 us -> 90.4 us (0.988)
  Pallas kernels: 90.7 us -> 89.6 us
    pallas_call x1, Pallas kernels: 88.8 us -> 87.7 us  [shards(): pl.pallas_call(functools.partial(kernel, geometry, tuple(shapes)), out_sh...]
where the time goes in v5:
time: 90.4 us; the launch traced here: 90.2 us
  Pallas kernels  89.6 us (99%)
    pallas_call x1, Pallas kernels, shards(): pl.pallas_call(functools.partial(kernel, geometry, tuple(shapes)), out_sh...  87.7 us
    pallas_call x1, Pallas kernels, shards(): pl.pallas_call(functools.partial(place, geometry), out_shape=(jax.ShapeDt...  1.87 us

profile of v5, /device:TPU:1, one launch (start us, length us, event | category | flops | bytes accessed | tf_op | source)
XLA Modules:
  0.0 90.2 jit_solution(18424274520979403873)
XLA Ops:
  0.6 87.7 %transport.1 = (f32[32,8,256]{2,1,0:T(8,128)}, f32[32,8,128]{2,1,0:T(8,128)}) custom-call(bf16[512,128]{1,0:T(8,128)(2,1)} %noise.1, bf16[128,512]{1,0:T(8,128)(2,1)} %w_first.1, bf16[512,1024]{1,0:T(8,128)(2,1)} %w_second_hbm.1, bf16[1024,1024]{1,0:T(8,128)(2,1)} %history_hbm.1), custom_call_target="tpu_custom_call" | custom-call | tf_op jit(solution)/shard_map/transport/pallas_call | solution.py:510
  88.4 1.9 %place.1 = (f32[128,512]{1,0:T(8,128)}, f32[64,512]{1,0:T(8,128)}) custom-call(f32[32,8,256]{2,1,0:T(8,128)} %get-tuple-element.6.first, f32[32,8,128]{2,1,0:T(8,128)} %get-tuple-element.7.second), custom_call_target="tpu_custom_call" | custom-call | tf_op jit(solution)/shard_map/place/pallas_call | solution.py:524

commit v6 on v5

--- a/solution.py
+++ b/solution.py
@@ -17,15 +17,19 @@
 LANES = 128
 
 
-def kernel(geometry, names, noise, w_first, w_second_hbm, history_hbm, out_first, out_second, *scratch):
+def kernel(geometry, names, noise_hbm, w_first_hbm, w_second_hbm, history_hbm, out_first, out_second, *scratch):
     ny, nx, nz = geometry
     chips = ny * nx
     n_row, n_col = 2 * chips, nz
     s = SimpleNamespace(**dict(zip(names, scratch)))
     sem = scratch[-1]
-    w_second, history = s.w_second, s.history
+    noise, w_first, w_second, history = s.noise, s.w_first, s.w_second, s.history
+    load_n = pltpu.make_async_copy(noise_hbm, noise, sem.at[76])
+    load_f = pltpu.make_async_copy(w_first_hbm, w_first, sem.at[77])
     load_w = pltpu.make_async_copy(w_second_hbm, w_second, sem.at[78])
     load_h = pltpu.make_async_copy(history_hbm, history, sem.at[79])
+    load_n.start()
+    load_f.start()
     load_w.start()
     load_h.start()
     gen, zdim = noise.shape
@@ -44,6 +48,7 @@
     x = lax.rem(chip, nx)
     y = chip // nx
     odd = lax.rem(z, 2) == 1
+    sibling = (me + 1 - 2 * core, z)
 
     barrier = pltpu.get_barrier_semaphore()
 
@@ -147,6 +152,9 @@
     tile_h = min(256, hid)
     tile_g = min(256, width)
     tile_j = min(256, hist)
+
+    load_n.wait()
+    load_f.wait()
 
     for n in range(hid // tile_h):
         cols = slice(n * tile_h, (n + 1) * tile_h)
@@ -285,6 +293,7 @@
         rows = block(k)
         for n, cols in enumerate(plan_tiles):
             v = s.plan[rows, cols] * s.col_b[n:n + 1, :]
+            s.plan[rows, cols] = v
             hi = v.astype(BF16)
             s.plan_hi[rows, cols] = hi
             s.plan_lo[rows, cols] = (v - hi.astype(F32)).astype(BF16)
@@ -321,11 +330,31 @@
         total = mine[...] + jnp.sum(theirs[...], axis=0)
         column_from_rows(1.0 / total, s.row_a)
 
+    for k in range(blocks):
+        for cols in tiles[:hid // LANES]:
+            rows = tiles[k]
+            d_hidden = (s.surf_w[rows, cols] * (1.0 / n_col) - s.value[rows, cols] * s.row_a[rows, :]) * scale
+            d_preact = d_hidden * s.mult[rows, cols]
+            hi = d_preact.astype(BF16)
+            s.d_hi[rows, cols] = hi
+            s.d_lo[rows, cols] = (d_preact - hi.astype(F32)).astype(BF16)
+    s.first[...] = dot(s.noise_t[...], s.d_hi[...]) + dot(s.noise_t[...], s.d_lo[...])
+    start(s.first.at[:, at(other * half, half, half)], s.first_in, 8, sibling)
+    expect(8, s.first_in)
+    piece = zdim // chips
+
+    def send_pieces():
+        arrived(8)
+        s.first_half[...] = s.first[:, at(core * half, half, half)] + s.first_in[...]
+        over_chips(lambda to, j: start(
+            s.first_half.at[at(to * piece, piece, 8), :], s.first_chip_in.at[j], 11, (to * 2 + core, z)))
+        expect(11, s.first_chip_in)
+
     def weight_rows(k):
         rows = block(k)
         own = s.row_a[rows, :]
-        for n, cols in enumerate(plan_tiles):
-            s.weights[rows, cols] = (s.plan[rows, cols] * own * s.col_b[n:n + 1, :]).astype(BF16)
+        for cols in plan_tiles:
+            s.weights[rows, cols] = (s.plan[rows, cols] * own).astype(BF16)
     for k in range(blocks):
         weight_rows(k)
 
@@ -339,7 +368,6 @@
 
     span_x, span_y = quarter // nx, quarter // ny
     base_u, base_l = core * half, core * half + quarter
-    sibling = (me + 1 - 2 * core, z)
     acc_tile(other)
     order = [pair for k in range(1, nx) for pair in ((True, k), (False, k))] + [(True, 0), (False, 0)]
 
@@ -379,28 +407,12 @@
         into = s.y_in2 if upper else s.x_in2
         start(s.acc.at[rows, :], into.at[k - 1], 13 if upper else 14, (chip_at(upper, k, False)[0], z))
 
-    for k in range(blocks):
-        for cols in tiles[:hid // LANES]:
-            rows = tiles[k]
-            d_hidden = (s.surf_w[rows, cols] * (1.0 / n_col) - s.value[rows, cols] * s.row_a[rows, :]) * scale
-            d_preact = d_hidden * s.mult[rows, cols]
-            hi = d_preact.astype(BF16)
-            s.d_hi[rows, cols] = hi
-            s.d_lo[rows, cols] = (d_preact - hi.astype(F32)).astype(BF16)
-    s.first[...] = dot(s.noise_t[...], s.d_hi[...]) + dot(s.noise_t[...], s.d_lo[...])
-    start(s.first.at[:, at(other * half, half, half)], s.first_in, 8, sibling)
-    expect(8, s.first_in)
+    send_pieces()
     acc_tile(core)
 
     for n in range(len(order)):
         pass_on(n)
 
-    arrived(8)
-    s.first_half[...] = s.first[:, at(core * half, half, half)] + s.first_in[...]
-    piece = zdim // chips
-    over_chips(lambda to, j: start(
-        s.first_half.at[at(to * piece, piece, 8), :], s.first_chip_in.at[j], 11, (to * 2 + core, z)))
-    expect(11, s.first_chip_in)
     for n in range(len(order) - 2):
         pass_second(n)
     expect(13, s.y_in2)
@@ -481,7 +493,7 @@
     piece = zdim // chips
     jr, ir = hist // LANES, gen // LANES
     shapes = dict(
-        w_second=((hid, width), BF16), history=((hist, width), BF16),
+        noise=((gen, zdim), BF16), w_first=((zdim, hid), BF16), w_second=((hid, width), BF16), history=((hist, width), BF16),
         hidden=((gen, hid), BF16), hidden_t=((hid, gen), BF16), noise_t=((zdim, gen), BF16),
         surface=((gen, width), BF16), mult=((gen, hid), F32), surf_w=((gen, hid), F32),
         hist_w_hi=((hist, hid), BF16), hist_w_lo=((hist, hid), BF16),
@@ -513,7 +525,7 @@
             jax.ShapeDtypeStruct((n_row, piece, half), F32),
             jax.ShapeDtypeStruct((n_row, 8, LANES), F32),
         ),
-        in_specs=[vmem] * 2 + [pl.BlockSpec(memory_space=pl.ANY)] * 2,
+        in_specs=[pl.BlockSpec(memory_space=pl.ANY)] * 4,
         out_specs=(vmem, vmem),
         scratch_shapes=scratch,
         compiler_params=pltpu.CompilerParams(

time: 90.4 us -> 88.8 us (0.982)
  Pallas kernels: 89.6 us -> 88.1 us
    pallas_call x1, Pallas kernels: 87.7 us -> 86.2 us  [shards(): pl.pallas_call(functools.partial(kernel, geometry, tuple(shapes)), out_sh...]
where the time goes in v6:
time: 88.8 us; the launch traced here: 88.7 us
  Pallas kernels  88.1 us (99%)
    pallas_call x1, Pallas kernels, shards(): pl.pallas_call(functools.partial(kernel, geometry, tuple(shapes)), out_sh...  86.2 us
    pallas_call x1, Pallas kernels, shards(): pl.pallas_call(functools.partial(place, geometry), out_shape=(jax.ShapeDt...  1.87 us

profile of v6, /device:TPU:1, one launch (start us, length us, event | category | flops | bytes accessed | tf_op | source)
XLA Modules:
  0.0 88.7 jit_solution(16046143381584695975)
XLA Ops:
  0.6 86.2 %transport.1 = (f32[32,8,256]{2,1,0:T(8,128)}, f32[32,8,128]{2,1,0:T(8,128)}) custom-call(bf16[512,128]{1,0:T(8,128)(2,1)} %noise_hbm.1, bf16[128,512]{1,0:T(8,128)(2,1)} %w_first_hbm.1, bf16[512,1024]{1,0:T(8,128)(2,1)} %w_second_hbm.1, bf16[1024,1024]{1,0:T(8,128)(2,1)} %history_hbm.1), custom_call_target="tpu_custom_call" | custom-call | tf_op jit(solution)/shard_map/transport/pallas_call | solution.py:522
  86.8 1.9 %place.1 = (f32[128,512]{1,0:T(8,128)}, f32[64,512]{1,0:T(8,128)}) custom-call(f32[32,8,256]{2,1,0:T(8,128)} %get-tuple-element.6.first, f32[32,8,128]{2,1,0:T(8,128)} %get-tuple-element.7.second), custom_call_target="tpu_custom_call" | custom-call | tf_op jit(solution)/shard_map/place/pallas_call | solution.py:536

commit v7 on v6

--- a/solution.py
+++ b/solution.py
@@ -413,13 +413,15 @@
     for n in range(len(order)):
         pass_on(n)
 
-    for n in range(len(order) - 2):
+    pass_second(0)
+    pass_second(1)
+    arrived(11)
+    s.first_piece[0] = s.first_half[at(chip * piece, piece, 8), :] + jnp.sum(s.first_chip_in[...], axis=0)
+    to_col(s.first_piece.at[0], s.first_z_in, 12)
+    for n in range(2, len(order) - 2):
         pass_second(n)
     expect(13, s.y_in2)
     expect(14, s.x_in2)
-    arrived(11)
-    s.first_piece[0] = s.first_half[at(chip * piece, piece, 8), :] + jnp.sum(s.first_chip_in[...], axis=0)
-    to_col(s.first_piece.at[0], s.first_z_in, 12)
     own_u, own_l = pass_second(len(order) - 2), pass_second(len(order) - 1)
     arrived(13)
     arrived(14)
@@ -458,21 +460,24 @@
     expect(17, s.second_all.at[pl.ds(0, n_row - 1)])
 
     arrived(16)
-    out_first[...] = s.first_all[...]
+    for k in range(chips):
+        for c in range(2):
+            out_first[k * piece:(k + 1) * piece, c * half:(c + 1) * half] = s.first_all[2 * k + c]
     arrived(17)
     out_second[...] = s.second_all[...]
     finish()
 
 
-def place(geometry, first, second, out_first, out_second, wide):
+def place(geometry, first, second, out_first, out_second, wide, done):
+    hand_on = pltpu.make_async_copy(first, out_first, done)
+    hand_on.start()
     ny, nx, nz = geometry
-    half, piece = out_first.shape[1] // 2, first.shape[1]
+    half = wide.shape[0] // 2
     quarter = half // 2
     for y in range(ny):
         for x in range(nx):
             chip = y * nx + x
             for c in range(2):
-                out_first[chip * piece:(chip + 1) * piece, c * half:(c + 1) * half] = first[2 * chip + c]
                 upper = c * half + y * (quarter // ny) + x * 8
                 lower = c * half + quarter + x * (quarter // nx) + y * 8
                 v = second[2 * chip + c]
@@ -480,6 +485,7 @@
                 wide[lower:lower + 8, :] = pltpu.roll(v, 64, axis=1)
     for k in range(wide.shape[0] // LANES):
         out_second[:, k * LANES:(k + 1) * LANES] = jnp.transpose(wide[k * LANES:(k + 1) * LANES, :])[0:64, :]
+    hand_on.wait()
 
 
 def shards(geometry, noise, w_first, w_second, history):
@@ -522,7 +528,7 @@
     first, second = pl.pallas_call(
         functools.partial(kernel, geometry, tuple(shapes)),
         out_shape=(
-            jax.ShapeDtypeStruct((n_row, piece, half), F32),
+            jax.ShapeDtypeStruct((zdim, hid), F32),
             jax.ShapeDtypeStruct((n_row, 8, LANES), F32),
         ),
         in_specs=[pl.BlockSpec(memory_space=pl.ANY)] * 4,
@@ -539,9 +545,9 @@
             jax.ShapeDtypeStruct((zdim, hid), F32),
             jax.ShapeDtypeStruct((width // nz, hid), F32),
         ),
-        in_specs=[vmem] * 2,
-        out_specs=(vmem, vmem),
-        scratch_shapes=[pltpu.VMEM((hid, LANES), F32)],
+        in_specs=[pl.BlockSpec(memory_space=pl.ANY), vmem],
+        out_specs=(pl.BlockSpec(memory_space=pl.ANY), vmem),
+        scratch_shapes=[pltpu.VMEM((hid, LANES), F32), pltpu.SemaphoreType.DMA],
         name="place",
     )(first, second)
     return grad_first, turned.T

time: 88.8 us -> 95.3 us (1.073)
  Pallas kernels: 88.1 us -> 94.5 us
    pallas_call x1, Pallas kernels: 1.87 us -> 10.6 us  [shards(): pl.pallas_call(functools.partial(place, geometry), out_shape=(jax.ShapeDt...]
    pallas_call x1, Pallas kernels: 86.2 us -> 83.9 us  [shards(): pl.pallas_call(functools.partial(kernel, geometry, tuple(shapes)), out_sh...]
where the time goes in v7:
time: 95.3 us; the launch traced here: 95.1 us
  Pallas kernels  94.5 us (99%)
    pallas_call x1, Pallas kernels, shards(): pl.pallas_call(functools.partial(kernel, geometry, tuple(shapes)), out_sh...  83.9 us
    pallas_call x1, Pallas kernels, shards(): pl.pallas_call(functools.partial(place, geometry), out_shape=(jax.ShapeDt...  10.6 us

profile of v7, /device:TPU:1, one launch (start us, length us, event | category | flops | bytes accessed | tf_op | source)
XLA Modules:
  0.0 95.1 jit_solution(3510087898437385669)
XLA Ops:
  0.6 83.9 %transport.1 = (f32[128,512]{1,0:T(8,128)}, f32[32,8,128]{2,1,0:T(8,128)}) custom-call(bf16[512,128]{1,0:T(8,128)(2,1)} %noise_hbm.1, bf16[128,512]{1,0:T(8,128)(2,1)} %w_first_hbm.1, bf16[512,1024]{1,0:T(8,128)(2,1)} %w_second_hbm.1, bf16[1024,1024]{1,0:T(8,128)(2,1)} %history_hbm.1), custom_call_target="tpu_custom_call" | custom-call | tf_op jit(solution)/shard_map/transport/pallas_call | solution.py:528
  84.5 10.6 %place.1 = (f32[128,512]{1,0:T(8,128)}, f32[64,512]{1,0:T(8,128)}) custom-call(f32[128,512]{1,0:T(8,128)} %get-tuple-element.6.first, f32[32,8,128]{2,1,0:T(8,128)} %get-tuple-element.7.second), custom_call_target="tpu_custom_call" | custom-call | tf_op jit(solution)/shard_map/place/pallas_call | solution.py:542

commit v8 on v7

--- a/solution.py
+++ b/solution.py
@@ -468,9 +468,8 @@
     finish()
 
 
-def place(geometry, first, second, out_first, out_second, wide, done):
-    hand_on = pltpu.make_async_copy(first, out_first, done)
-    hand_on.start()
+def place(geometry, first, second, out_first, out_second, wide):
+    out_first[...] = first[...]
     ny, nx, nz = geometry
     half = wide.shape[0] // 2
     quarter = half // 2
@@ -485,7 +484,6 @@
                 wide[lower:lower + 8, :] = pltpu.roll(v, 64, axis=1)
     for k in range(wide.shape[0] // LANES):
         out_second[:, k * LANES:(k + 1) * LANES] = jnp.transpose(wide[k * LANES:(k + 1) * LANES, :])[0:64, :]
-    hand_on.wait()
 
 
 def shards(geometry, noise, w_first, w_second, history):
@@ -545,9 +543,9 @@
             jax.ShapeDtypeStruct((zdim, hid), F32),
             jax.ShapeDtypeStruct((width // nz, hid), F32),
         ),
-        in_specs=[pl.BlockSpec(memory_space=pl.ANY), vmem],
-        out_specs=(pl.BlockSpec(memory_space=pl.ANY), vmem),
-        scratch_shapes=[pltpu.VMEM((hid, LANES), F32), pltpu.SemaphoreType.DMA],
+        in_specs=[vmem] * 2,
+        out_specs=(vmem, vmem),
+        scratch_shapes=[pltpu.VMEM((hid, LANES), F32)],
         name="place",
     )(first, second)
     return grad_first, turned.T

time: 95.3 us -> 86.5 us (0.908)
  Pallas kernels: 94.5 us -> 85.7 us
    pallas_call x1, Pallas kernels: 10.6 us -> 1.87 us  [shards(): pl.pallas_call(functools.partial(place, geometry), out_shape=(jax.ShapeDt...]
where the time goes in v8:
time: 86.5 us; the launch traced here: 86.4 us
  Pallas kernels  85.7 us (99%)
    pallas_call x1, Pallas kernels, shards(): pl.pallas_call(functools.partial(kernel, geometry, tuple(shapes)), out_sh...  83.9 us
    pallas_call x1, Pallas kernels, shards(): pl.pallas_call(functools.partial(place, geometry), out_shape=(jax.ShapeDt...  1.87 us

profile of v8, /device:TPU:1, one launch (start us, length us, event | category | flops | bytes accessed | tf_op | source)
XLA Modules:
  0.0 86.4 jit_solution(6174163308705554578)
XLA Ops:
  0.6 83.9 %transport.1 = (f32[128,512]{1,0:T(8,128)}, f32[32,8,128]{2,1,0:T(8,128)}) custom-call(bf16[512,128]{1,0:T(8,128)(2,1)} %noise_hbm.1, bf16[128,512]{1,0:T(8,128)(2,1)} %w_first_hbm.1, bf16[512,1024]{1,0:T(8,128)(2,1)} %w_second_hbm.1, bf16[1024,1024]{1,0:T(8,128)(2,1)} %history_hbm.1), custom_call_target="tpu_custom_call" | custom-call | tf_op jit(solution)/shard_map/transport/pallas_call | solution.py:526
  84.5 1.9 %place.1 = (f32[128,512]{1,0:T(8,128)}, f32[64,512]{1,0:T(8,128)}) custom-call(f32[128,512]{1,0:T(8,128)} %get-tuple-element.6.first, f32[32,8,128]{2,1,0:T(8,128)} %get-tuple-element.7.second), custom_call_target="tpu_custom_call" | custom-call | tf_op jit(solution)/shard_map/place/pallas_call | solution.py:540

commit v9 on v8

--- a/solution.py
+++ b/solution.py
@@ -413,12 +413,10 @@
     for n in range(len(order)):
         pass_on(n)
 
-    pass_second(0)
-    pass_second(1)
     arrived(11)
     s.first_piece[0] = s.first_half[at(chip * piece, piece, 8), :] + jnp.sum(s.first_chip_in[...], axis=0)
     to_col(s.first_piece.at[0], s.first_z_in, 12)
-    for n in range(2, len(order) - 2):
+    for n in range(len(order) - 2):
         pass_second(n)
     expect(13, s.y_in2)
     expect(14, s.x_in2)

time: 86.5 us -> 86.5 us (level)
  no operation moved by 1% of the time
where the time goes in v9:
time: 86.5 us; the launch traced here: 86.4 us
  Pallas kernels  85.7 us (99%)
    pallas_call x1, Pallas kernels, shards(): pl.pallas_call(functools.partial(kernel, geometry, tuple(shapes)), out_sh...  83.9 us
    pallas_call x1, Pallas kernels, shards(): pl.pallas_call(functools.partial(place, geometry), out_shape=(jax.ShapeDt...  1.87 us

profile of v9, /device:TPU:1, one launch (start us, length us, event | category | flops | bytes accessed | tf_op | source)
XLA Modules:
  0.0 86.4 jit_solution(13496395264291600298)
XLA Ops:
  0.6 83.9 %transport.1 = (f32[128,512]{1,0:T(8,128)}, f32[32,8,128]{2,1,0:T(8,128)}) custom-call(bf16[512,128]{1,0:T(8,128)(2,1)} %noise_hbm.1, bf16[128,512]{1,0:T(8,128)(2,1)} %w_first_hbm.1, bf16[512,1024]{1,0:T(8,128)(2,1)} %w_second_hbm.1, bf16[1024,1024]{1,0:T(8,128)(2,1)} %history_hbm.1), custom_call_target="tpu_custom_call" | custom-call | tf_op jit(solution)/shard_map/transport/pallas_call | solution.py:524
  84.5 1.9 %place.1 = (f32[128,512]{1,0:T(8,128)}, f32[64,512]{1,0:T(8,128)}) custom-call(f32[128,512]{1,0:T(8,128)} %get-tuple-element.6.first, f32[32,8,128]{2,1,0:T(8,128)} %get-tuple-element.7.second), custom_call_target="tpu_custom_call" | custom-call | tf_op jit(solution)/shard_map/place/pallas_call | solution.py:538
